TPU v7x, 32 devices: a whole 2x2x4 slice. The times are simulated.
32 devices in a mesh: task: 2 (over x), batch: 16 (over z, y, core).
Axes of the slice: x: 2, y: 2, z: 4, core: 2. Of those that a mesh axis runs over, the one named last changes fastest.
Arguments:
- inputs: bfloat16 [2, 128, 256, 2048], P('task', 'batch')
- crop_cuts: int32 [2, 128, 2], P('task', 'batch'), may hold values from 2 to 13
- threshold: bfloat16 [2, 128, 256, 2048], P('task', 'batch'), may hold values from 0 to 1
- w_reduce: bfloat16 [2048, 512], replicated, may hold values from -0.125 to 0.125
- w_spatial: bfloat16 [9, 512, 512], replicated, may hold values from -0.09375 to 0.09375
- w_expand: bfloat16 [512, 2048], replicated, may hold values from -0.25 to 0.25
- w_heads: bfloat16 [2, 2048, 256], P('task'), may hold values from -0.125 to 0.125
- gain_one: float32 [512], replicated, may hold values from 0.1 to 1.9
- bias_one: float32 [512], replicated, may hold values from -3 to 3
- gain_two: float32 [512], replicated, may hold values from 0.1 to 1.9
- bias_two: float32 [512], replicated, may hold values from -3 to 3
- gain_three: float32 [2048], replicated, may hold values from 0.1 to 1.9
- bias_three: float32 [2048], replicated, may hold values from -3 to 3
- cotangent: bfloat16 [2, 2, 128, 256, 256], P('task', None, 'batch')
Outputs:
- heads: float32 [2, 2, 128, 256, 256], P('task', None, 'batch')
- grad_inputs: bfloat16 [2, 128, 256, 2048], P('task', 'batch')
- grad_reduce: float32 [2048, 512], replicated
- grad_spatial: float32 [9, 512, 512], replicated
- grad_expand: float32 [512, 2048], replicated
- grad_heads: float32 [2, 2048, 256], P('task')
- grad_gain_one: float32 [512], replicated
- grad_bias_one: float32 [512], replicated
- grad_gain_two: float32 [512], replicated
- grad_bias_two: float32 [512], replicated
- grad_gain_three: float32 [2048], replicated
- grad_bias_three: float32 [2048], replicated
Inputs may be any that keep to these rules, and one draw needn't show every extreme that they name: `crop_cuts`: each entry is a row cut followed by a column cut of its canvas.
All inputs are finite; a program needn't handle non-finite values.
Results may differ from a plain program's by a relative error of at most 0.014.
Values may be sent and summed in bfloat16 or wider, within the bound.
A program may use at most 384 MiB of HBM per device.

v0:
```python
import jax
import jax.numpy as jnp
from jax import lax
from jax.sharding import PartitionSpec as P

SIDE = 16


OFFSETS = ((-1, -1), (-1, 0), (-1, 1), (0, -1), (0, 0), (0, 1), (1, -1), (1, 0), (1, 1))
EPS = 1e-05
FLOOR = 0.1
SOFT = 0.25
ROOT_HALF = 0.7071067811865476
DENSITY = 0.3989422804014327
CONTRACT_ROWS = (((0,), (0,)), ((), ()))
CONTRACT_COLS = (((1,), (1,)), ((), ()))


def smooth(value):
    return jax.nn.gelu(value, approximate=False)


def slope(value):
    return (
        0.5 * (1.0 + lax.erf(value * ROOT_HALF)) + value * jnp.exp(-0.5 * value * value) * DENSITY
    )


def displace(array, down, right, first, fill):
    widths = [(0, 0)] * array.ndim
    widths[first] = (1, 1)
    widths[first + 1] = (1, 1)
    padded = jnp.pad(array, widths, constant_values=fill)
    rows_here = array.shape[first]
    cols_here = array.shape[first + 1]
    padded = lax.slice_in_dim(padded, 1 + down, 1 + down + rows_here, axis=first)
    return lax.slice_in_dim(padded, 1 + right, 1 + right + cols_here, axis=first + 1)


def tap_valid(cuts, side):
    lines = jnp.arange(side, dtype=jnp.int32)
    upper = (lines[None, :, None] >= cuts[:, 0, None, None]).astype(jnp.int32)
    left = (lines[None, None, :] >= cuts[:, 1, None, None]).astype(jnp.int32)
    ident = upper * 2 + left
    return [ident == displace(ident, down, right, 1, -1) for down, right in OFFSETS]


def spatial_forward(flat, weights, valid, canvases):
    grid = flat.reshape(canvases, SIDE, SIDE, -1)
    total = jnp.zeros((flat.shape[0], weights.shape[2]), jnp.float32)
    for index, (down, right) in enumerate(OFFSETS):
        moved = jnp.where(
            valid[index][..., None], displace(grid, down, right, 1, 0), jnp.zeros((), flat.dtype)
        )
        total = total + jnp.dot(
            moved.reshape(flat.shape), weights[index], preferred_element_type=jnp.float32
        )
    return total


def spatial_backward(flat, grad_low, weights, valid, canvases):
    grid = flat.reshape(canvases, SIDE, SIDE, -1)
    upstream = grad_low.reshape(canvases, SIDE, SIDE, -1)
    back = jnp.zeros(grid.shape, jnp.float32)
    weight_terms = []
    for index, (down, right) in enumerate(OFFSETS):
        moved = jnp.where(
            valid[index][..., None], displace(grid, down, right, 1, 0), jnp.zeros((), flat.dtype)
        )
        weight_terms.append(
            lax.dot_general(
                moved.reshape(flat.shape),
                grad_low,
                CONTRACT_ROWS,
                preferred_element_type=jnp.float32,
            )
        )
        masked = jnp.where(valid[index][..., None], upstream, jnp.zeros((), grad_low.dtype))
        piece = lax.dot_general(
            masked.reshape(grad_low.shape),
            weights[index],
            CONTRACT_COLS,
            preferred_element_type=jnp.float32,
        )
        back = back + displace(piece.reshape(grid.shape), -down, -right, 1, 0.0)
    return (jnp.stack(weight_terms), back.reshape(flat.shape))


def norm_forward(hidden, gain, bias, count):
    centre = lax.psum(jnp.sum(hidden, axis=0), ("task", "batch")) / count
    spread = lax.psum(jnp.sum(jnp.square(hidden - centre), axis=0), ("task", "batch")) / count
    scale = lax.rsqrt(spread + EPS)
    normed = (hidden - centre) * scale
    return (normed * gain + bias, normed, scale)


def norm_backward(upstream, normed, scale, gain, count):
    bias_grad, gain_grad = lax.psum(
        (jnp.sum(upstream, axis=0), jnp.sum(upstream * normed, axis=0)), ("task", "batch")
    )
    hidden_grad = gain * scale * (upstream - bias_grad / count - normed * gain_grad / count)
    return (hidden_grad.astype(jnp.bfloat16), gain_grad, bias_grad)


def keep_share(grads, limit):
    purity = 0.5 * (
        1.0 + jnp.sum(grads, axis=0) / jnp.maximum(jnp.sum(jnp.abs(grads), axis=0), FLOOR)
    )
    return jnp.clip((purity - limit) / SOFT + 0.5, 0.0, 1.0)


def body(
    inputs,
    crop_cuts,
    threshold,
    w_reduce,
    w_spatial,
    w_expand,
    w_heads,
    gain_one,
    bias_one,
    gain_two,
    bias_two,
    gain_three,
    bias_three,
    cotangent,
):
    canvases = inputs.shape[1]
    pixels = inputs.shape[2]
    width = inputs.shape[3]
    rows = canvases * pixels
    out_width = w_heads.shape[2]
    count = lax.axis_size("task") * lax.axis_size("batch") * rows
    valid = tap_valid(crop_cuts.reshape(canvases, 2), SIDE)
    flat_in = inputs.reshape(rows, width)
    h_one = jnp.dot(flat_in, w_reduce, preferred_element_type=jnp.float32)
    n_one, xh_one, inv_one = norm_forward(h_one, gain_one, bias_one, count)
    q_one = smooth(n_one).astype(jnp.bfloat16)
    h_two = spatial_forward(q_one, w_spatial, valid, canvases)
    n_two, xh_two, inv_two = norm_forward(h_two, gain_two, bias_two, count)
    q_two = smooth(n_two).astype(jnp.bfloat16)
    h_three = jnp.dot(q_two, w_expand, preferred_element_type=jnp.float32)
    n_three, xh_three, inv_three = norm_forward(h_three, gain_three, bias_three, count)
    before = n_three + flat_in.astype(jnp.float32)
    trunk_low = smooth(before).astype(jnp.bfloat16)
    everyone = lax.all_gather(
        trunk_low.reshape(1, canvases, pixels, width), "task", axis=0, tiled=True
    )
    wide = everyone.reshape(-1, width)
    head_out = jnp.dot(wide, w_heads[0], preferred_element_type=jnp.float32).reshape(
        1, -1, canvases, pixels, out_width
    )
    upstream = cotangent.reshape(-1, out_width)
    head_local = lax.dot_general(wide, upstream, CONTRACT_ROWS, preferred_element_type=jnp.float32)
    task_grad = lax.dot_general(
        upstream, w_heads[0], CONTRACT_COLS, preferred_element_type=jnp.float32
    ).astype(jnp.bfloat16)
    both_grads, both_limits = (
        lax.all_gather(
            task_grad.reshape(1, -1, canvases, pixels, width), "task", axis=0, tiled=True
        ),
        lax.all_gather(threshold, "task", axis=0, tiled=True),
    )
    grads_float = both_grads.astype(jnp.float32)
    keep = keep_share(grads_float, both_limits.astype(jnp.float32))
    own = lax.dynamic_index_in_dim(grads_float, lax.axis_index("task"), 0, keepdims=False)
    term = jnp.where(own > 0, keep * own, (1.0 - keep) * own)
    merged = (
        lax.psum_scatter(term.astype(jnp.bfloat16), "task", scatter_dimension=0, tiled=True)
        .astype(jnp.float32)
        .reshape(rows, width)
    )
    grad_heads = lax.psum(head_local, "batch")[None]
    flow = merged * slope(before)
    dh_three, dg_three, db_three = norm_backward(flow, xh_three, inv_three, gain_three, count)
    grad_expand = lax.dot_general(
        q_two, dh_three, CONTRACT_ROWS, preferred_element_type=jnp.float32
    )
    dq_two = lax.dot_general(dh_three, w_expand, CONTRACT_COLS, preferred_element_type=jnp.float32)
    dh_two, dg_two, db_two = norm_backward(dq_two * slope(n_two), xh_two, inv_two, gain_two, count)
    grad_spatial, dq_one = spatial_backward(q_one, dh_two, w_spatial, valid, canvases)
    dh_one, dg_one, db_one = norm_backward(dq_one * slope(n_one), xh_one, inv_one, gain_one, count)
    grad_reduce = lax.dot_general(
        flat_in, dh_one, CONTRACT_ROWS, preferred_element_type=jnp.float32
    )
    grad_inputs = (
        flow + lax.dot_general(dh_one, w_reduce, CONTRACT_COLS, preferred_element_type=jnp.float32)
    ).astype(jnp.bfloat16)
    grad_expand, grad_spatial, grad_reduce = lax.psum(
        (grad_expand, grad_spatial, grad_reduce), ("task", "batch")
    )
    return (
        head_out,
        grad_inputs.reshape(inputs.shape),
        grad_reduce,
        grad_spatial,
        grad_expand,
        grad_heads,
        dg_one,
        db_one,
        dg_two,
        db_two,
        dg_three,
        db_three,
    )


def solution(mesh):
    in_specs = (
        P("task", "batch", None, None),
        P("task", "batch", None),
        P("task", "batch", None, None),
        P(),
        P(),
        P(),
        P("task", None, None),
        P(),
        P(),
        P(),
        P(),
        P(),
        P(),
        P("task", None, "batch", None, None),
    )
    out_specs = (
        P("task", None, "batch", None, None),
        P("task", "batch", None, None),
        P(),
        P(),
        P(),
        P("task", None, None),
        P(),
        P(),
        P(),
        P(),
        P(),
        P(),
    )
    return jax.shard_map(body, mesh=mesh, in_specs=in_specs, out_specs=out_specs, check_vma=False)
```

profile of v0, /device:TPU:0, one launch (start us, length us, event | category | flops | bytes accessed | tf_op | source)
XLA Modules:
  0.0 1906.7 jit_solution(5200170576455485648)
XLA Ops:
  8.8 9.3 convolution_convert_fusion
  19.0 390.6 %all-gather.6.cloned.1.call-done = bf16[2,2,8,256,2048]{4,3,2,1,0:T(8,128)(2,1)} async-done(((bf16[1,2,8,256,2048]{4,3,2,1,0:T(8,128)(2,1)}), bf16[2,2,8,256,2048]{4,3,2,1,0:T(8,128)(2,1)}) %all-gather.6.cloned.1.call-update) | async-done | bytes 33554448 | tf_op jit(solution)/shard_map/all_gather | solution.py:159
  409.6 34.8 %convert_element_type.71 = f32[2,2,8,256,2048]{4,3,2,1,0:T(8,128)} convert(bf16[2,2,8,256,2048]{4,3,2,1,0:T(8,128)(2,1)} %all-gather.6.cloned.1.call-done) | non-fusion elementwise | flops 16777216 | bytes 100663296 | tf_op jit(solution)/shard_map/convert_element_type | solution.py:164
  444.4 31.9 %convert_reduce_fusion = f32[2,8,256,2048]{3,2,1,0:T(8,128)} fusion(bf16[2,2,8,256,2048]{4,3,2,1,0:T(8,128)(2,1)} %all-gather.6.cloned.1.call-done), kind=kLoop, calls=%fused_computation.6 | loop fusion | flops 25165824 | bytes 67108864 | tf_op jit(solution)/shard_map/reduce_sum | solution.py:107
  476.3 32.2 %abs_reduce_fusion = f32[2,8,256,2048]{3,2,1,0:T(8,128)} fusion(bf16[2,2,8,256,2048]{4,3,2,1,0:T(8,128)(2,1)} %all-gather.6.cloned.1.call-done), kind=kLoop, calls=%fused_computation | loop fusion | flops 41943040 | bytes 67108864 | tf_op jit(solution)/shard_map/reduce_sum | solution.py:107
  508.5 101.5 %all-gather.8.cloned.1.call-done = bf16[2,8,256,2048]{3,2,1,0:T(8,128)(2,1)} async-done(((bf16[1,8,256,2048]{3,2,1,0:T(8,128)(2,1)}), bf16[2,8,256,2048]{3,2,1,0:T(8,128)(2,1)}) %all-gather.8.cloned.1.call-update) | async-done | bytes 16777232 | tf_op jit(solution)/shard_map/all_gather | solution.py:162
  610.0 43.4 %fusion.1 = bf16[2,8,256,2048]{3,2,1,0:T(8,128)(2,1)} fusion(bf16[2,8,256,2048]{3,2,1,0:T(8,128)(2,1)} %all-gather.8.cloned.1.call-done, f32[2,8,256,2048]{3,2,1,0:T(8,128)} %convert_reduce_fusion, f32[2,8,256,2048]{3,2,1,0:T(8,128)} %abs_reduce_fusion, f32[2,2,8,256,2048]{4,3,2,1,0:T(8,128)} %convert_element_type.71, s32[]{:T(128)S(6)} %select_n.85), kind=kLoop, calls=%fused_computation.5 | loop fusion | flops 125829120 | bytes 134217728 | tf_op jit(solution)/shard_map/convert_element_type | solution.py:169
  655.4 10.5 fusion.136
  665.9 39.9 %psum.112 = f32[512]{0:T(512)S(1)} all-reduce(f32[512]{0:T(512)S(1)} %get-tuple-element.87), channel_id=1, replica_groups=mesh['task'=2,'batch'=16] {'task','batch'}, use_global_device_ids=true, to_apply=%region_1.2 | all-reduce | flops 512 | bytes 4096 | tf_op jit(solution)/shard_map/psum | solution.py:90
  708.5 41.4 %psum.113 = f32[512]{0:T(512)S(1)} all-reduce(f32[512]{0:T(512)S(1)} %multiply_reduce_fusion.5), channel_id=1, replica_groups=mesh['task'=2,'batch'=16] {'task','batch'}, use_global_device_ids=true, to_apply=%region_3.4 | all-reduce | flops 512 | bytes 4096 | tf_op jit(solution)/shard_map/psum | solution.py:91
  751.0 11.0 fusion.19
  764.9 7.0 fusion.62
  773.3 3.8 fusion.102
  793.3 12.1 fusion.137
  805.4 40.2 %psum.114 = f32[512]{0:T(512)S(1)} all-reduce(f32[512]{0:T(512)S(1)} %get-tuple-element.89), channel_id=1, replica_groups=mesh['task'=2,'batch'=16] {'task','batch'}, use_global_device_ids=true, to_apply=%region_5.6 | all-reduce | flops 512 | bytes 4096 | tf_op jit(solution)/shard_map/psum | solution.py:90
  848.5 40.5 %psum.115 = f32[512]{0:T(512)S(1)} all-reduce(f32[512]{0:T(512)S(1)} %multiply_reduce_fusion.4), channel_id=1, replica_groups=mesh['task'=2,'batch'=16] {'task','batch'}, use_global_device_ids=true, to_apply=%region_7.8 | all-reduce | flops 512 | bytes 4096 | tf_op jit(solution)/shard_map/psum | solution.py:91
  889.0 11.1 fusion.22
  900.2 8.3 fusion.138
  908.4 39.4 %psum.116 = f32[2048]{0:T(1024)S(1)} all-reduce(f32[2048]{0:T(1024)S(1)} %get-tuple-element.91), channel_id=1, replica_groups=mesh['task'=2,'batch'=16] {'task','batch'}, use_global_device_ids=true, to_apply=%region_9.10 | all-reduce | flops 2048 | bytes 16384 | tf_op jit(solution)/shard_map/psum | solution.py:90
  947.9 7.5 multiply_reduce_fusion.1
  955.4 40.7 %psum.117 = f32[2048]{0:T(1024)S(1)} all-reduce(f32[2048]{0:T(1024)S(1)} %multiply_reduce_fusion.1), channel_id=1, replica_groups=mesh['task'=2,'batch'=16] {'task','batch'}, use_global_device_ids=true, to_apply=%region_11.12 | all-reduce | flops 2048 | bytes 16384 | tf_op jit(solution)/shard_map/psum | solution.py:91
  996.2 51.4 %fusion.131 = (f32[2048]{0:T(1024)S(1)}, f32[2048]{0:T(1024)S(1)}, f32[2048,2048]{1,0:T(8,128)}, bf16[2048,2048]{1,0:T(8,128)(2,1)}) fusion(f32[2048]{0:T(1024)S(1)} %get-tuple-element.80, f32[2048,2048]{1,0:T(8,128)} %get-tuple-element.92, f32[2048]{0:T(1024)S(1)} %broadcast_multiply_fusion.1, bf16[1,8,256,2048]{3,2,1,0:T(8,128)(2,1)} %param.14, ...), kind=kLoop, calls=%fused_computation.250 | loop fusion | flops 352317440 | bytes 58769408 | tf_op jit(solution)/shard_map/reduce_sum | solution.py:99
  1047.5 40.0 %all-reduce.12 = (f32[2048]{0:T(1024)S(1)}, f32[2048]{0:T(1024)S(1)}) all-reduce(f32[2048]{0:T(1024)S(1)} %get-tuple-element.37, f32[2048]{0:T(1024)S(1)} %get-tuple-element.36), channel_id=1, replica_groups=mesh['task'=2,'batch'=16] {'task','batch'}, use_global_device_ids=true, to_apply=%region_18.19 | all-reduce | flops 4096 | bytes 32768 | tf_op jit(solution)/shard_map/psum | solution.py:98
  1087.5 12.9 multiply_convert_fusion
  1100.5 7.8 fusion.133
  1108.3 6.2 fusion.139
  1114.5 40.7 %all-reduce.11 = (f32[512]{0:T(512)S(1)}, f32[512]{0:T(512)S(1)}) all-reduce(f32[512]{0:T(512)S(1)} %get-tuple-element.41, f32[512]{0:T(512)S(1)} %get-tuple-element.40), channel_id=1, replica_groups=mesh['task'=2,'batch'=16] {'task','batch'}, use_global_device_ids=true, to_apply=%region_22.23 | all-reduce | flops 1024 | bytes 8192 | tf_op jit(solution)/shard_map/psum | solution.py:98
  1155.2 4.3 broadcast_select_fusion
  1186.2 3.3 fusion.78
  1189.5 3.3 fusion.80
  1192.9 3.3 fusion.83
  1196.2 3.4 fusion.85
  1199.5 3.4 fusion.87
  1202.9 3.4 fusion.89
  1206.2 3.4 fusion.74
  1209.7 14.8 fusion.40
  1224.5 6.2 fusion.132
  1230.7 39.5 %all-reduce.10 = (f32[512]{0:T(512)S(1)}, f32[512]{0:T(512)S(1)}) all-reduce(f32[512]{0:T(512)S(1)} %get-tuple-element.39, f32[512]{0:T(512)S(1)} %get-tuple-element.38), channel_id=1, replica_groups=mesh['task'=2,'batch'=16] {'task','batch'}, use_global_device_ids=true, to_apply=%region_26.27 | all-reduce | flops 1024 | bytes 8192 | tf_op jit(solution)/shard_map/psum | solution.py:98
  1270.2 4.6 multiply_convert_fusion.1
  1276.2 9.4 convolution_bitcast_fusion
  1286.3 16.2 add_convert_fusion
  1302.5 275.9 %all-reduce.19.cloned.1.call-done = (f32[2048,512]{0,1:T(8,128)}, f32[9,512,512]{2,1,0:T(8,128)}, f32[512,2048]{1,0:T(8,128)}) async-done(((f32[2048,512]{0,1:T(8,128)}, f32[9,512,512]{2,1,0:T(8,128)}, f32[512,2048]{1,0:T(8,128)}), (f32[2048,512]{0,1:T(8,128)}, f32[9,512,512]{2,1,0:T(8,128)}, f32[512,2048]{1,0:T(8,128)})) %all-reduce.19.cloned.1.call-update) | async-done | bytes 17825808 | tf_op jit(solution)/shard_map/psum | solution.py:189
  1578.4 5.6 copy.27
  1583.9 194.6 %all-gather.4.cloned.1.call-done = bf16[2,8,256,2048]{3,2,1,0:T(8,128)(2,1)} async-done(((bf16[1,8,256,2048]{3,2,1,0:T(8,128)(2,1)}), bf16[2,8,256,2048]{3,2,1,0:T(8,128)(2,1)}) %all-gather.4.cloned.1.call-update) | async-done | bytes 16777232 | tf_op jit(solution)/shard_map/all_gather | solution.py:146
  1778.5 9.8 convolution_bitcast_fusion.1
  1788.3 10.3 convolution_bitcast_fusion.2
  1798.6 87.7 %all-reduce.17.cloned.1.call-done = f32[1,2048,256]{2,1,0:T(8,128)} async-done(((f32[1,2048,256]{2,1,0:T(8,128)}), f32[1,2048,256]{2,1,0:T(8,128)}) %all-reduce.17.cloned.1.call-update) | async-done | bytes 2097168 | tf_op jit(solution)/shard_map/psum | solution.py:173
  1886.3 8.7 copy.50
  (165 shorter events, 64.4 us)
Async XLA Ops:
  7.2 402.4 %all-gather.6.cloned.1.call-start = ((), (), s32[]{:S(2)}) async-start(), calls=%async_computation.2 | async-start | bytes 50331648 | tf_op jit(solution)/shard_map/all_gather | solution.py:159
  18.1 591.9 %all-gather.8.cloned.1.call-start = ((), (), s32[]{:S(2)}) async-start(), calls=%async_computation.3 | async-start | bytes 25165824 | tf_op jit(solution)/shard_map/all_gather | solution.py:162
  18.9 977.2 %reduce-scatter.2.cloned.1.call-start = ((), (), s32[]{:S(2)}) async-start(), calls=%async_computation.4 | async-start | bytes 25165824 | tf_op jit(solution)/shard_map/reduce_scatter | solution.py:169
  653.5 924.9 %all-reduce.19.cloned.1.call-start = ((), (), s32[]{:S(2)}) async-start(), calls=%async_computation.6 | async-start | bytes 35651584 | tf_op jit(solution)/shard_map/psum | solution.py:189
  665.9 84.0 %copy-start.32 = (f32[512]{0:T(512)S(1)}, f32[512]{0:T(512)}, u32[]{:S(2)}) copy-start(f32[512]{0:T(512)} %param.21) | copy-start | bytes 6148
  665.9 85.2 %copy-start.35 = (f32[512]{0:T(512)S(1)}, f32[512]{0:T(512)}, u32[]{:S(2)}) copy-start(f32[512]{0:T(512)} %param.22) | copy-start | bytes 6148
  705.7 56.3 %copy-start.27 = (f32[512]{0:T(512)}, f32[512]{0:T(512)S(1)}, u32[]{:S(2)}) copy-start(f32[512]{0:T(512)S(1)} %broadcast_multiply_fusion.5) | copy-start | bytes 6148
  762.0 2.8 copy-start.2
  762.0 9.9 slice-start
  764.9 7.1 slice-start.1
  771.9 5.2 copy-start.15
  771.9 8.4 copy-start.13
  771.9 8.4 copy-start.17
  772.0 11.6 copy-start.5
  772.0 14.8 copy-start.7
  772.0 18.1 copy-start.9
  772.0 21.3 %copy-start.19 = (bf16[8,16,16,512]{3,2,1,0:T(8,128)(2,1)}, bf16[8,16,16,512]{3,2,1,0:T(8,128)(2,1)S(1)}, u32[]{:S(2)}) copy-start(bf16[8,16,16,512]{3,2,1,0:T(8,128)(2,1)S(1)} %get-tuple-element.63) | copy-start | bytes 6291460
  805.4 83.6 %copy-start.37 = (f32[512]{0:T(512)S(1)}, f32[512]{0:T(512)}, u32[]{:S(2)}) copy-start(f32[512]{0:T(512)} %param.23) | copy-start | bytes 6148
  805.4 83.6 %copy-start.41 = (f32[512]{0:T(512)S(1)}, f32[512]{0:T(512)}, u32[]{:S(2)}) copy-start(f32[512]{0:T(512)} %param.24) | copy-start | bytes 6148
  889.0 11.2 copy-start.47
  900.2 8.3 copy-start.23
  947.9 48.2 %copy-start.31 = (f32[2048]{0:T(1024)S(1)}, f32[2048]{0:T(1024)}, u32[]{:S(2)}) copy-start(f32[2048]{0:T(1024)} %param.25) | copy-start | bytes 24580
  947.9 48.3 %copy-start.40 = (f32[2048]{0:T(1024)S(1)}, f32[2048]{0:T(1024)}, u32[]{:S(2)}) copy-start(f32[2048]{0:T(1024)} %param.26) | copy-start | bytes 24580
  1087.5 13.0 copy-start.34
  1087.5 13.0 copy-start.39
  1087.5 13.0 copy-start.1
  1087.5 13.0 copy-start.48
  1100.5 7.8 copy-start.24
  1155.1 4.3 copy-start.42
  1155.1 4.3 copy-start.44
  1155.1 4.3 copy-start.18
  1159.5 20.6 %copy-start.4 = (bf16[2048,512]{1,0:T(8,128)(2,1)}, bf16[2048,512]{1,0:T(8,128)(2,1)S(1)}, u32[]{:S(2)}) copy-start(bf16[2048,512]{1,0:T(8,128)(2,1)S(1)} %get-tuple-element.53) | copy-start | bytes 6291460
  1159.5 2.5 copy-start.16
  1162.0 2.3 copy-start.14
  1177.9 5.0 slice-start.2
  1180.1 2.8 slice-start.3
  1209.6 14.8 copy-start.28
  1209.6 14.9 copy-start.30
  1209.6 14.9 copy-start.33
  1209.6 14.9 copy-start.36
  1224.5 45.7 %copy-start.38 = (f32[512]{0:T(512)S(1)}, f32[512]{0:T(512)}, u32[]{:S(2)}) copy-start(f32[512]{0:T(512)} %get-tuple-element.81) | copy-start | bytes 6148
  1270.2 4.6 copy-start.43
  1270.2 4.7 copy-start.45
  1285.6 492.9 %all-gather.4.cloned.1.call-start = ((), (), s32[]{:S(2)}) async-start(), calls=%async_computation.1 | async-start | bytes 25165824 | tf_op jit(solution)/shard_map/all_gather | solution.py:146
  1286.2 600.0 %all-reduce.17.cloned.1.call-start = ((), (), s32[]{:S(2)}) async-start(), calls=%async_computation.5 | async-start | bytes 4194304 | tf_op jit(solution)/shard_map/psum | solution.py:173
  1778.5 9.8 copy-start.26
  1886.3 8.7 copy-start.21
  1895.0 3.1 copy-start.25
  (11 other events, 19.1 us)
Sparse Core Ops, SparseCore 0:
  18.3 391.2 all-gather.5
  411.1 198.8 all-gather.7
  653.6 193.3 reduce-scatter.1
  1285.8 292.5 all-reduce.18
  1579.8 198.7 all-gather.3
  1788.4 97.7 all-reduce.16
where the time goes:
time: 1920 us; the launch traced here: 1910 us
  waiting for transfers between devices  1050 us (55%)
  blocking collectives  362 us (19%)
  other arithmetic  268 us (14%)
  matrix products  186 us (10%)
  local copies, waits for them, and re-layouts  23.7 us (1%)
    all_gather x1, waiting for transfers between devices, body(): lax.all_gather(task_grad.reshape(1, -1, canvases, pixels, width), 'task',...  391 us
    psum x1, waiting for transfers between devices, body(): lax.psum((grad_expand, grad_spatial, grad_reduce), ('task', 'batch'))  276 us
    all_gather x1, waiting for transfers between devices, body(): lax.all_gather(trunk_low.reshape(1, canvases, pixels, width), 'task', axi...  195 us
    psum x3, blocking collectives, norm_forward(): lax.psum(jnp.sum(jnp.square(hidden - centre), axis=0), ('task', 'batch'))  123 us
    psum x3, blocking collectives, norm_backward(): lax.psum((jnp.sum(upstream, axis=0), jnp.sum(upstream * normed, axis=0)),...  120 us
    psum x3, blocking collectives, norm_forward(): centre = lax.psum(jnp.sum(hidden, axis=0), ('task', 'batch')) / count  120 us
    all_gather x1, waiting for transfers between devices, body(): lax.all_gather(threshold, 'task', axis=0, tiled=True)  101 us
    psum x1, waiting for transfers between devices, body(): grad_heads = lax.psum(head_local, 'batch')[None]  87.7 us
  transfers between devices with their start and end apart: 6, of which 5 were waited for; matrix products, arithmetic and copies ran while one was open for 12% of the time, Pallas kernels for 0%

commit v1 on v0

v1 whole, which is shorter than its diff:
```python
import functools

import jax
import jax.numpy as jnp
from jax import lax
from jax.experimental import pallas as pl
from jax.experimental.pallas import tpu as pltpu
from jax.sharding import PartitionSpec as P

SIDE = 16
EPS = 1e-05
FLOOR = 0.1
SOFT = 0.25
ROOT_HALF = 0.7071067811865476
DENSITY = 0.3989422804014327
ROWS_ROWS = (((0,), (0,)), ((), ()))
COLS_COLS = (((1,), (1,)), ((), ()))
MESH = pl.DeviceIdType.MESH
LOW = 4


def bulk(value):
    return 0.5 * (1.0 + lax.erf(value * ROOT_HALF))


def slope(value):
    return bulk(value) + value * jnp.exp(-0.5 * value * value) * DENSITY


def centred_join(total, spread, share):
    groups = total.shape[0]
    whole = jnp.sum(total, axis=0)
    means = total / share
    centre = whole / (share * groups)
    return whole, jnp.sum(spread, axis=0) + share * jnp.sum(jnp.square(means - centre), axis=0)


def stats_kernel(rows, forward, tasks, batch, local, out, near, far, middle, near_send, near_recv, far_send, far_recv):
    task = lax.axis_index("task")
    place = lax.axis_index("batch")
    high = place // LOW
    low = lax.rem(place, LOW)
    near_size = tasks * LOW
    far_size = batch // LOW
    me_near = task * LOW + low

    def near_peer(step):
        slot = lax.rem(me_near + step, near_size)
        return slot, (slot // LOW, high * LOW + lax.rem(slot, LOW))

    def far_peer(step):
        slot = lax.rem(high + step, far_size)
        return slot, (task, slot * LOW + low)

    def join(held, count, share):
        half = local.shape[0] // 2
        total = held[:, :half]
        spread = held[:, half:]
        if forward:
            return centred_join(total, spread, share)
        return jnp.sum(total, axis=0), jnp.sum(spread, axis=0)

    barrier = pltpu.get_barrier_semaphore()
    for step in range(1, near_size):
        pl.semaphore_signal(barrier, inc=1, device_id=near_peer(step)[1], device_id_type=MESH)
    for step in range(1, far_size):
        pl.semaphore_signal(barrier, inc=1, device_id=far_peer(step)[1], device_id_type=MESH)
    pl.semaphore_wait(barrier, near_size + far_size - 2)

    def run(size, peer, me, source, held, send, recv):
        copies = []
        for step in range(1, size):
            slot, device = peer(step)
            copy = pltpu.make_async_remote_copy(
                src_ref=source,
                dst_ref=held.at[me],
                send_sem=send.at[step],
                recv_sem=recv.at[me],
                device_id=device,
                device_id_type=MESH,
            )
            copy.start()
            copies.append(copy)
        for step in range(1, size):
            slot, device = peer(step)
            pltpu.make_async_remote_copy(
                src_ref=source,
                dst_ref=held.at[slot],
                send_sem=send.at[step],
                recv_sem=recv.at[slot],
                device_id=device,
                device_id_type=MESH,
            ).wait_recv()
        for copy in copies:
            copy.wait_send()

    half = local.shape[0] // 2
    near[me_near] = local[...]
    run(near_size, near_peer, me_near, local, near, near_send, near_recv)
    total, spread = join(near[...], near_size, float(rows))
    middle[:half] = total
    middle[half:] = spread
    far[high] = middle[...]
    run(far_size, far_peer, high, middle, far, far_send, far_recv)
    total, spread = join(far[...], far_size, float(rows * near_size))
    out[:half] = total
    out[half:] = spread


def reduce_stats(first, second, rows, forward, ident):
    tasks = lax.axis_size("task")
    batch = lax.axis_size("batch")
    width = first.shape[0]
    local = jnp.concatenate([first.reshape(-1, 128), second.reshape(-1, 128)], axis=0)
    shape = local.shape
    near_size = tasks * LOW
    far_size = batch // LOW
    out = pl.pallas_call(
        functools.partial(stats_kernel, rows, forward, tasks, batch),
        out_shape=jax.ShapeDtypeStruct(shape, jnp.float32),
        in_specs=[pl.BlockSpec(memory_space=pltpu.VMEM)],
        out_specs=pl.BlockSpec(memory_space=pltpu.VMEM),
        scratch_shapes=[
            pltpu.VMEM((near_size,) + shape, jnp.float32),
            pltpu.VMEM((far_size,) + shape, jnp.float32),
            pltpu.VMEM(shape, jnp.float32),
            pltpu.SemaphoreType.DMA((near_size,)),
            pltpu.SemaphoreType.DMA((near_size,)),
            pltpu.SemaphoreType.DMA((far_size,)),
            pltpu.SemaphoreType.DMA((far_size,)),
        ],
        compiler_params=pltpu.CompilerParams(collective_id=ident, has_side_effects=True),
        name="stats_%d" % ident,
    )(local)
    half = shape[0] // 2
    return out[:half].reshape(width), out[half:].reshape(width)


def norm_forward(hidden, gain, bias, ident):
    rows = hidden.shape[0]
    count = lax.axis_size("task") * lax.axis_size("batch") * rows
    total = jnp.sum(hidden, axis=0)
    spread = jnp.sum(jnp.square(hidden - total / rows), axis=0)
    total, spread = reduce_stats(total, spread, rows, True, ident)
    centre = total / count
    scale = lax.rsqrt(spread / count + EPS)
    normed = (hidden - centre) * scale
    return normed * gain + bias, normed, scale


def norm_backward(upstream, normed, scale, gain, ident):
    rows = upstream.shape[0]
    count = lax.axis_size("task") * lax.axis_size("batch") * rows
    bias_grad, gain_grad = reduce_stats(
        jnp.sum(upstream, axis=0), jnp.sum(upstream * normed, axis=0), rows, False, ident
    )
    hidden_grad = gain * scale * (upstream - bias_grad / count - normed * gain_grad / count)
    return hidden_grad.astype(jnp.bfloat16), gain_grad, bias_grad


def moved(array, down, right):
    rows, cols = array.shape[1:3]
    padded = jnp.pad(array, ((0, 0), (1, 1), (1, 1), (0, 0)))
    return padded[:, 1 + down : 1 + down + rows, 1 + right : 1 + right + cols]


def body(
    inputs,
    crop_cuts,
    threshold,
    w_reduce,
    w_spatial,
    w_expand,
    w_heads,
    gain_one,
    bias_one,
    gain_two,
    bias_two,
    gain_three,
    bias_three,
    cotangent,
):
    low = jnp.bfloat16
    full = jnp.float32
    canvases, pixels, width = inputs.shape[1:]
    mid = w_reduce.shape[1]
    rows = canvases * pixels
    out_width = w_heads.shape[2]
    task = lax.axis_index("task")
    swap = [(0, 1), (1, 0)]
    cot = cotangent.reshape(2, rows, out_width)
    cot_mine = lax.dynamic_index_in_dim(cot, task, 0, keepdims=False)
    cot_send = lax.dynamic_index_in_dim(cot, 1 - task, 0, keepdims=False)
    cot_peer = lax.ppermute(cot_send, "task", swap)
    heads_mine = w_heads[0]
    heads_peer = lax.ppermute(heads_mine, "task", swap)

    lines = jnp.arange(SIDE, dtype=jnp.int32)
    cuts = crop_cuts.reshape(canvases, 2)
    row_edge = lines[None, :] == cuts[:, 0:1]
    col_edge = lines[None, :] == cuts[:, 1:2]
    from_above = jnp.logical_not(row_edge | (lines == 0)[None, :]).astype(low)
    from_left = jnp.logical_not(col_edge | (lines == 0)[None, :]).astype(low)
    from_below = jnp.pad(from_above[:, 1:], ((0, 0), (0, 1)))
    from_right = jnp.pad(from_left[:, 1:], ((0, 0), (0, 1)))
    by_row = lambda mask: mask[:, :, None, None]
    by_col = lambda mask: mask[:, None, :, None]

    flat_in = inputs.reshape(rows, width)
    h_one = jnp.dot(flat_in, w_reduce, preferred_element_type=full)
    n_one, xh_one, inv_one = norm_forward(h_one, gain_one, bias_one, 0)
    q_one = (n_one * bulk(n_one)).astype(low).reshape(canvases, SIDE, SIDE, mid)
    sides = jnp.concatenate(
        [moved(q_one, 0, -1) * by_col(from_left), q_one, moved(q_one, 0, 1) * by_col(from_right)],
        axis=-1,
    )
    taps = w_spatial.reshape(3, 3 * mid, mid)
    h_two = (
        jnp.dot((moved(sides, -1, 0) * by_row(from_above)).reshape(rows, -1), taps[0], preferred_element_type=full)
        + jnp.dot(sides.reshape(rows, -1), taps[1], preferred_element_type=full)
        + jnp.dot((moved(sides, 1, 0) * by_row(from_below)).reshape(rows, -1), taps[2], preferred_element_type=full)
    )
    n_two, xh_two, inv_two = norm_forward(h_two, gain_two, bias_two, 1)
    q_two = (n_two * bulk(n_two)).astype(low)
    h_three = jnp.dot(q_two, w_expand, preferred_element_type=full)
    n_three, xh_three, inv_three = norm_forward(h_three, gain_three, bias_three, 2)
    before = n_three + flat_in.astype(full)
    trunk = (before * bulk(before)).astype(low)

    out_mine = jnp.dot(trunk, heads_mine, preferred_element_type=full)
    out_sent = jnp.dot(trunk, heads_peer, preferred_element_type=full).astype(low)
    out_peer = lax.ppermute(out_sent, "task", swap).astype(full)
    first = jnp.where(task == 0, out_mine, out_peer)
    second = jnp.where(task == 0, out_peer, out_mine)
    head_out = jnp.stack([first, second]).reshape(1, 2, canvases, pixels, out_width)

    grad_mine = lax.dot_general(trunk, cot_mine, ROWS_ROWS, preferred_element_type=full)
    grad_sent = lax.dot_general(trunk, cot_peer, ROWS_ROWS, preferred_element_type=full)
    grad_other = lax.ppermute(grad_sent.astype(low), "task", swap).astype(full)
    grad_heads = lax.psum((grad_mine + grad_other).astype(low), "batch").astype(full)[None]

    g_mine = lax.dot_general(cot_mine, heads_mine, COLS_COLS, preferred_element_type=full)
    g_peer = lax.dot_general(cot_peer, heads_peer, COLS_COLS, preferred_element_type=full)
    g_mine = g_mine.astype(low).astype(full)
    g_peer = g_peer.astype(low).astype(full)
    both = g_mine + g_peer
    size = jnp.abs(g_mine) + jnp.abs(g_peer)
    purity = 0.5 * (1.0 + both / jnp.maximum(size, FLOOR))
    keep = jnp.clip((purity - threshold.reshape(rows, width).astype(full)) / SOFT + 0.5, 0.0, 1.0)
    merged = 0.5 * (both - size) + keep * size

    flow = merged * slope(before)
    dh_three, dg_three, db_three = norm_backward(flow, xh_three, inv_three, gain_three, 3)
    grad_expand = lax.dot_general(q_two, dh_three, ROWS_ROWS, preferred_element_type=full)
    grad_expand = lax.psum(grad_expand.astype(low), ("task", "batch")).astype(full)
    dq_two = lax.dot_general(dh_three, w_expand, COLS_COLS, preferred_element_type=full)
    dh_two, dg_two, db_two = norm_backward(dq_two * slope(n_two), xh_two, inv_two, gain_two, 4)
    up = dh_two.reshape(canvases, SIDE, SIDE, mid)
    lanes = jnp.concatenate(
        [moved(up * by_row(from_above), 1, 0), up, moved(up * by_row(from_below), -1, 0)], axis=-1
    ).reshape(rows, 3 * mid)
    across = w_spatial.reshape(3, 3, mid, mid)
    pieces = [
        lax.dot_general(
            lanes,
            across[:, b].transpose(1, 0, 2).reshape(mid, 3 * mid),
            COLS_COLS,
            preferred_element_type=full,
        ).reshape(up.shape)
        for b in range(3)
    ]
    dq_one = (
        pieces[1]
        + moved(pieces[0] * by_col(from_left).astype(full), 0, 1)
        + moved(pieces[2] * by_col(from_right).astype(full), 0, -1)
    ).reshape(rows, mid)
    dh_one, dg_one, db_one = norm_backward(dq_one * slope(n_one), xh_one, inv_one, gain_one, 5)
    grad_spatial = lax.dot_general(
        sides.reshape(rows, 3 * mid), lanes, ROWS_ROWS, preferred_element_type=full
    )
    grad_spatial = lax.psum(grad_spatial.astype(low), ("task", "batch"))
    grad_spatial = (
        grad_spatial.reshape(3, mid, 3, mid).transpose(2, 0, 1, 3).reshape(w_spatial.shape).astype(full)
    )
    grad_reduce = lax.dot_general(flat_in, dh_one, ROWS_ROWS, preferred_element_type=full)
    grad_reduce = lax.psum(grad_reduce.astype(low), ("task", "batch")).astype(full)
    grad_inputs = (
        flow + lax.dot_general(dh_one, w_reduce, COLS_COLS, preferred_element_type=full)
    ).astype(low)
    return (
        head_out,
        grad_inputs.reshape(inputs.shape),
        grad_reduce,
        grad_spatial,
        grad_expand,
        grad_heads,
        dg_one,
        db_one,
        dg_two,
        db_two,
        dg_three,
        db_three,
    )


def solution(mesh):
    in_specs = (
        P("task", "batch", None, None),
        P("task", "batch", None),
        P("task", "batch", None, None),
        P(),
        P(),
        P(),
        P("task", None, None),
        P(),
        P(),
        P(),
        P(),
        P(),
        P(),
        P("task", None, "batch", None, None),
    )
    out_specs = (
        P("task", None, "batch", None, None),
        P("task", "batch", None, None),
        P(),
        P(),
        P(),
        P("task", None, None),
        P(),
        P(),
        P(),
        P(),
        P(),
        P(),
    )
    return jax.shard_map(body, mesh=mesh, in_specs=in_specs, out_specs=out_specs, check_vma=False)
```

time: 1920 us -> 645 us (0.34)
  waiting for transfers between devices: 1050 us -> 230 us
  blocking collectives: 362 us -> 0 us
  other arithmetic: 268 us -> 85.3 us
  Pallas kernels: 0 us -> 94 us
  matrix products: 186 us -> 155 us
  local copies, waits for them, and re-layouts: 23.7 us -> 54.6 us
    all_gather x3 -> x0, waiting for transfers between devices: 687 us -> none  [the longest x1 391 us: body(): lax.all_gather(task_grad.reshape(1, -1, canvases, pixels, width), 'task',...]
    psum x9 -> x0, blocking collectives: 362 us -> none  [the longest x3 123 us: norm_forward(): lax.psum(jnp.sum(jnp.square(hidden - centre), axis=0), ('task', 'batch'))]
    psum x2, waiting for transfers between devices: 364 us -> 206 us  [the longest x1 189 us: body(): lax.psum(grad_reduce.astype(low), ('task', 'batch')).astype(full)]
    pallas_call x0 -> x6, Pallas kernels: none -> 94 us  [reduce_stats(): pl.pallas_call(functools.partial(stats_kernel, rows, forward, tasks, batc...]
    convert_element_type x5 -> x7, other arithmetic: 100 us -> 27.3 us  [the longest x1 11.7 us: body(): trunk = (before * bulk(before)).astype(low)]
    reduce_sum x5 -> x3, other arithmetic: 77.1 us -> 8.63 us  [norm_forward(): spread = jnp.sum(jnp.square(hidden - total / rows), axis=0)]
    reduce_sum x2 -> x1, other arithmetic: 57.5 us -> 3.96 us  [norm_backward(): jnp.sum(upstream, axis=0)]
    dot_general x36 -> x19, matrix products: 186 us -> 155 us  [the longest x1 27.4 us: body(): lax.dot_general(cot_peer, heads_peer, COLS_COLS, preferred_element_type=f...]
  transfers between devices with their start and end apart: 6 -> 6, of which waited for: 5 -> 4; matrix products, arithmetic and copies ran while one was open for 12% -> 27% of each run, Pallas kernels for 0% -> 10%
where the time goes in v1:
time: 645 us; the launch traced here: 638 us
  waiting for transfers between devices  230 us (36%)
  matrix products  155 us (24%)
  Pallas kernels  94 us (15%)
  other arithmetic  85.3 us (13%)
  local copies, waits for them, and re-layouts  54.6 us (8%)
  between operations  15 us (2%)
    psum x1, waiting for transfers between devices, body(): lax.psum(grad_reduce.astype(low), ('task', 'batch')).astype(full)  189 us
    pallas_call x6, Pallas kernels, reduce_stats(): pl.pallas_call(functools.partial(stats_kernel, rows, forward, tasks, batc...  94 us
    dot_general x1, matrix products, body(): lax.dot_general(cot_peer, heads_peer, COLS_COLS, preferred_element_type=f...  27.4 us
    convert_element_type x2, local copies, waits for them, and re-layouts, body(): grad_spatial.reshape(3, mid, 3, mid).transpose(2, 0, 1, 3)  18 us
    psum x1, waiting for transfers between devices, body(): lax.psum((grad_mine + grad_other).astype(low), 'batch').astype(full)[None]  17 us
    unnamed x115, local copies, waits for them, and re-layouts  16.6 us
    dot_general x1, matrix products, body(): lax.dot_general(sides.reshape(rows, 3 * mid), lanes, ROWS_ROWS, preferred...  15.6 us
    convert_element_type x3, other arithmetic, norm_backward(): return (hidden_grad.astype(jnp.bfloat16), gain_grad, bias_grad)  15.3 us
  transfers between devices with their start and end apart: 6, of which 4 were waited for; matrix products, arithmetic and copies ran while one was open for 27% of the time, Pallas kernels for 10%

profile of v1, /device:TPU:0, one launch (start us, length us, event | category | flops | bytes accessed | tf_op | source)
XLA Modules:
  0.0 638.3 jit_solution(7078800734398470990)
XLA Ops:
  9.9 2.9 collective-permute-start.2
  12.8 7.6 %fusion.64 = (f32[512]{0:T(512)S(1)}, f32[2048,512]{1,0:T(8,128)S(1)}) fusion(bf16[2048,2048]{1,0:T(8,128)(2,1)} %bitcast.158, bf16[2048,512]{1,0:T(8,128)(2,1)} %param.17), kind=kOutput, calls=%fused_computation.148 | convolution fusion | flops 4296015360 | bytes 14682112 | tf_op jit(solution)/shard_map/dot_general | solution.py:210
  23.5 42.5 %stats_0.1 = f32[8,128]{1,0:T(8,128)} custom-call(f32[8,128]{1,0:T(8,128)} %pad_maximum_fusion.5.local), custom_call_target="tpu_custom_call" | custom-call | tf_op jit(solution)/shard_map/stats_0/pallas_call | solution.py:118
  68.3 2.9 fusion.63
  75.3 5.0 pad_maximum_fusion
  80.4 4.2 fusion.11
  84.6 3.4 fusion.67
  88.1 3.4 fusion.68
  91.5 3.5 fusion.65
  98.2 10.1 %stats_1.1 = f32[8,128]{1,0:T(8,128)} custom-call(f32[8,128]{1,0:T(8,128)} %pad_maximum_fusion.6.local), custom_call_target="tpu_custom_call" | custom-call | tf_op jit(solution)/shard_map/stats_1/pallas_call | solution.py:118
  109.8 2.9 multiply_convert_fusion.4
  112.8 8.8 %fusion.66 = (f32[2048]{0:T(1024)S(1)}, f32[2048,2048]{1,0:T(8,128)}) fusion(bf16[2048,512]{1,0:T(8,128)(2,1)S(1)} %multiply_convert_fusion.4, bf16[512,2048]{1,0:T(8,128)(2,1)S(1)} %copy-done.55), kind=kOutput, calls=%fused_computation.150 | convolution fusion | flops 4299159552 | bytes 20979712 | tf_op jit(solution)/shard_map/dot_general | solution.py:225
  121.6 7.6 %multiply_reduce_fusion.1 = f32[2048]{0:T(1024)S(1)} fusion(f32[2048,2048]{1,0:T(8,128)} %get-tuple-element.98, f32[2048]{0:T(1024)S(1)} %broadcast_multiply_fusion.3), kind=kLoop, calls=%fused_computation.23 | loop fusion | flops 12580864 | bytes 16793600 | tf_op jit(solution)/shard_map/reduce_sum | solution.py:143
  129.8 10.7 %stats_2.1 = f32[32,128]{1,0:T(8,128)} custom-call(f32[32,128]{1,0:T(8,128)} %pad_maximum_fusion.3.local), custom_call_target="tpu_custom_call" | custom-call | tf_op jit(solution)/shard_map/stats_2/pallas_call | solution.py:118
  141.2 6.6 %fusion.39 = bf16[2048,2048]{1,0:T(8,128)(2,1)} fusion(bf16[2,2048,256]{2,1,0:T(8,128)(2,1)S(1)} %bitcast.144, s32[]{:T(128)S(6)} %select_n.22, bf16[1,2048,256]{2,1,0:T(8,128)(2,1)S(1)} %copy-done.30), kind=kOutput, calls=%fused_computation.91 | convolution fusion | flops 2147483648 | bytes 10485764 | tf_op jit(solution)/shard_map/dot_general | solution.py:242
  147.9 5.5 slice_bitcast_fusion.2
  153.4 11.7 %multiply_convert_fusion.1 = (bf16[2048,2048]{1,0:T(8,128)(2,1)}, f32[2048,2048]{1,0:T(8,128)}) fusion(bf16[1,8,256,2048]{3,2,1,0:T(8,128)(2,1)} %param.14, f32[2048]{0:T(1024)S(1)} %copy-done.50, f32[2048]{0:T(1024)S(1)} %copy-done.40, f32[2048]{0:T(1024)S(1)} %get-tuple-element.81, f32[2048,2048]{1,0:T(8,128)S(1)} %copy-done.2, f32[2048]{0:T(1024)S(1)} %get-tuple-element.80), kind=kLoop, calls=%fused_computation.19 | loop fusion | flops 46137344 | bytes 50364416 | tf_op jit(solution)/shard_map/convert_element_type | solution.py:228
  165.1 2.6 copy.39
  167.7 2.6 copy.37
  170.4 2.6 copy.35
  173.0 7.4 %fusion.37 = f32[2048,256]{1,0:T(8,128)} fusion(bf16[2048,2048]{1,0:T(8,128)(2,1)} %get-tuple-element.64, bf16[2,2048,256]{2,1,0:T(8,128)(2,1)S(1)} %bitcast.146, s32[]{:T(128)S(6)} %select_n.22), kind=kOutput, calls=%fused_computation.89 | convolution fusion | flops 2147483648 | bytes 11534340 | tf_op jit(solution)/shard_map/dot_general | solution.py:237
  181.9 27.4 %fusion.59 = (f32[2048]{0:T(1024)S(1)}, f32[2048]{0:T(1024)S(1)}, f32[2048,2048]{1,0:T(8,128)}) fusion(f32[2048]{0:T(1024)S(1)} %get-tuple-element.81, f32[2048,2048]{1,0:T(8,128)} %get-tuple-element.98, f32[2048]{0:T(1024)S(1)} %get-tuple-element.80, f32[2048,2048]{1,0:T(8,128)S(1)} %copy-done.13, bf16[1,8,256,2048]{3,2,1,0:T(8,128)(2,1)} %param.16, ...), kind=kOutput, calls=%fused_computation.144 | convolution fusion | flops 2290085888 | bytes 69238784 | tf_op jit(solution)/shard_map/dot_general | solution.py:243
  209.9 10.3 %stats_3.1 = f32[32,128]{1,0:T(8,128)} custom-call(f32[32,128]{1,0:T(8,128)} %pad_maximum_fusion.4.local), custom_call_target="tpu_custom_call" | custom-call | tf_op jit(solution)/shard_map/stats_3/pallas_call | solution.py:118
  222.2 12.9 %multiply_convert_fusion = bf16[2048,2048]{1,0:T(8,128)(2,1)S(1)} fusion(f32[2048,2048]{1,0:T(8,128)} %get-tuple-element.99, f32[2048,2048]{1,0:T(8,128)} %get-tuple-element.98, f32[2048]{0:T(1024)S(1)} %slice_bitcast_fusion.3, f32[2048]{0:T(1024)S(1)} %get-tuple-element.62, f32[2048]{0:T(1024)S(1)} %fusion.58, f32[2048]{0:T(1024)S(1)} %get-tuple-element.81, ...), kind=kLoop, calls=%fused_computation.17 | loop fusion | flops 33554432 | bytes 41984000 | tf_op jit(solution)/shard_map/convert_element_type | solution.py:158
  235.2 7.8 %fusion.61 = (f32[512]{0:T(512)S(1)}, f32[512]{0:T(512)S(1)}, f32[2048,512]{1,0:T(8,128)}) fusion(f32[512]{0:T(512)S(1)} %get-tuple-element.83, f32[2048,512]{1,0:T(8,128)S(1)} %copy-done.8, f32[512]{0:T(512)S(1)} %get-tuple-element.82, f32[512]{0:T(512)S(1)} %copy-done.53, f32[512]{0:T(512)S(1)} %copy-done.47, ...), kind=kOutput, calls=%fused_computation.146 | convolution fusion | flops 4311743488 | bytes 18886656 | tf_op jit(solution)/shard_map/dot_general | solution.py:256
  243.6 10.3 %stats_4.1 = f32[8,128]{1,0:T(8,128)} custom-call(f32[8,128]{1,0:T(8,128)} %pad_maximum_fusion.7.local), custom_call_target="tpu_custom_call" | custom-call | tf_op jit(solution)/shard_map/stats_4/pallas_call | solution.py:118
  255.9 9.5 %convolution_convert_fusion = bf16[512,2048]{1,0:T(8,128)(2,1)} fusion(bf16[2048,512]{1,0:T(8,128)(2,1)S(1)} %copy-done.24, bf16[2048,2048]{1,0:T(8,128)(2,1)} %copy-done.14), kind=kOutput, calls=%fused_computation.73 | convolution fusion | flops 4296015872 | bytes 12582912 | tf_op jit(solution)/shard_map/dot_general | solution.py:254
  269.6 3.5 convolution_multiply_fusion
  273.1 4.9 convolution_multiply_fusion.1
  278.1 5.9 fusion.30
  284.1 4.0 fusion.60
  288.6 10.0 %stats_5.1 = f32[8,128]{1,0:T(8,128)} custom-call(f32[8,128]{1,0:T(8,128)} %pad_maximum_fusion.8.local), custom_call_target="tpu_custom_call" | custom-call | tf_op jit(solution)/shard_map/stats_5/pallas_call | solution.py:118
  300.7 6.3 convolution_convert_fusion.2
  310.2 9.2 %fusion.33 = bf16[2048,512]{0,1:T(8,128)(2,1)} fusion(bf16[2048,512]{1,0:T(8,128)(2,1)S(1)} %multiply_convert_fusion.2, bf16[2048,2048]{1,0:T(8,128)(2,1)} %bitcast.159), kind=kOutput, calls=%fused_computation.75 | convolution fusion | flops 4296015872 | bytes 12582912 | tf_op jit(solution)/shard_map/dot_general | solution.py:285
  319.5 11.9 %collective-permute-done.3 = bf16[2048,256]{1,0:T(8,128)(2,1)S(1)} collective-permute-done((bf16[2048,256]{1,0:T(8,128)(2,1)S(1)}, bf16[2048,256]{1,0:T(8,128)(2,1)S(1)}, u32[]{:S(2)}, u32[]{:S(2)}) %collective-permute-start.3) | collective-permute-done | bytes 1048608 | tf_op jit(solution)/shard_map/ppermute | solution.py:239
  332.7 15.6 %bitcast_convert_fusion = bf16[1536,1536]{1,0:T(8,128)(2,1)} fusion(bf16[8,16,16,512]{3,2,1,0:T(8,128)(2,1)} %copy-done.17, bf16[8,16,16,512]{3,2,1,0:T(8,128)(2,1)S(1)} %bitcast.152, bf16[8,16,16,512]{3,2,1,0:T(8,128)(2,1)} %copy-done.16, bf16[8,16,16,512]{3,2,1,0:T(8,128)(2,1)} %copy-done.25, bf16[8,16,16,512]{3,2,1,0:T(8,128)(2,1)} %bitcast.157, ...), kind=kOutput, calls=%fused_computation.26 | convolution fusion | flops 9703784448 | bytes 17301504 | tf_op jit(solution)/shard_map/dot_general | solution.py:278
  348.3 11.8 %convert_element_type.155 = bf16[3,512,3,512]{3,2,1,0:T(4,128)(2,1)} reshape(bf16[1536,1536]{1,0:T(8,128)(2,1)} %bitcast_convert_fusion) | data formatting | bytes 9437184 | tf_op jit(solution)/shard_map/convert_element_type | solution.py:283
  360.2 6.2 copy.41
  367.6 5.9 fusion.53
  373.5 7.1 %convolution_convert_fusion.3 = bf16[2048,256]{1,0:T(8,128)(2,1)} fusion(bf16[2048,2048]{1,0:T(8,128)(2,1)} %get-tuple-element.64, bf16[2048,256]{1,0:T(8,128)(2,1)} %collective-permute-done), kind=kOutput, calls=%fused_computation.79 | convolution fusion | flops 2148007936 | bytes 10485760 | tf_op jit(solution)/shard_map/dot_general | solution.py:231
  381.2 11.0 %add_convert_fusion = bf16[2048,2048]{1,0:T(8,128)(2,1)} fusion(f32[2048,2048]{1,0:T(8,128)} %get-tuple-element.99, bf16[2048,512]{1,0:T(8,128)(2,1)S(1)} %copy-done.20, bf16[2048,512]{1,0:T(8,128)(2,1)} %param.17), kind=kOutput, calls=%fused_computation.16 | convolution fusion | flops 4303355904 | bytes 29360128 | tf_op jit(solution)/shard_map/dot_general | solution.py:288
  392.2 12.1 %collective-permute-done.1 = bf16[2048,256]{1,0:T(8,128)(2,1)} collective-permute-done((bf16[2048,256]{1,0:T(8,128)(2,1)}, bf16[2048,256]{1,0:T(8,128)(2,1)}, u32[]{:S(2)}, u32[]{:S(2)}) %collective-permute-start.1) | collective-permute-done | bytes 1048608 | tf_op jit(solution)/shard_map/ppermute | solution.py:232
  408.3 17.0 %all-reduce.12.cloned.1.call-done = bf16[1,2048,256]{2,1,0:T(8,128)(2,1)} async-done(((bf16[1,2048,256]{2,1,0:T(8,128)(2,1)}), bf16[1,2048,256]{2,1,0:T(8,128)(2,1)}) %all-reduce.12.cloned.1.call-update) | async-done | bytes 1048592 | tf_op jit(solution)/shard_map/psum | solution.py:240
  425.3 2.7 broadcast_in_dim.6
  428.0 189.1 %all-reduce.14.cloned.1.call-done = (bf16[2048,512]{0,1:T(8,128)(2,1)}, bf16[9,512,512]{2,1,0:T(8,128)(2,1)}, bf16[512,2048]{1,0:T(8,128)(2,1)}) async-done(((bf16[2048,512]{0,1:T(8,128)(2,1)}, bf16[9,512,512]{2,1,0:T(8,128)(2,1)}, bf16[512,2048]{1,0:T(8,128)(2,1)}), (bf16[2048,512]{0,1:T(8,128)(2,1)}, bf16[9,512,512]{2,1,0:T(8,128)(2,1)}, bf16[512,2048]{1,0:T(8,128)(2,1)})) %all-reduce.14.cloned.1.call-update) | async-done | bytes 8912912 | tf_op jit(solution)/shard_map/psum | solution.py:286
  617.1 7.5 %convert_element_type.158 = f32[9,512,512]{2,1,0:T(8,128)} convert(bf16[9,512,512]{2,1,0:T(8,128)(2,1)} %get-tuple-element.55) | non-fusion elementwise | flops 2359296 | bytes 14155776 | tf_op jit(solution)/shard_map/convert_element_type | solution.py:283
  624.6 2.5 convert_element_type.160
  627.1 4.1 copy.42
  (163 shorter events, 42.0 us)
Async XLA Ops:
  7.2 418.1 %all-reduce.12.cloned.1.call-start = ((), (), s32[]{:S(2)}) async-start(), calls=%async_computation | async-start | bytes 2097152 | tf_op jit(solution)/shard_map/psum | solution.py:240
  9.9 170.5 %collective-permute-start.2 = (bf16[2048,256]{1,0:T(8,128)(2,1)}, bf16[2048,256]{1,0:T(8,128)(2,1)}, u32[]{:S(2)}, u32[]{:S(2)}) collective-permute-start(bf16[2048,256]{1,0:T(8,128)(2,1)} %dynamic-slice_bitcast_fusion), channel_id=1, source_target_pairs={{0,16},{16,0},{1,17},{17,1},{2,18},{18,2},{3,19},{19,3},{4,20},{20... | collective-permute-start | bytes 3145736 | tf_op jit(solution)/shard_map/ppermute | solution.py:194
  12.8 167.6 %collective-permute-start = (bf16[2048,256]{1,0:T(8,128)(2,1)}, bf16[2048,256]{1,0:T(8,128)(2,1)}, u32[]{:S(2)}, u32[]{:S(2)}) collective-permute-start(bf16[2048,256]{1,0:T(8,128)(2,1)} %bitcast.172), channel_id=1, source_target_pairs={{0,16},{16,0},{1,17},{17,1},{2,18},{18,2},{3,19},{19,3},{4,20},{20... | collective-permute-start | bytes 3145736 | tf_op jit(solution)/shard_map/ppermute | solution.py:196
  20.4 46.4 %copy-start.54 = (s32[1,8,2]{1,2,0:T(2,128)S(1)}, s32[1,8,2]{1,2,0:T(2,128)}, u32[]{:S(2)}) copy-start(s32[1,8,2]{1,2,0:T(2,128)} %param.15) | copy-start | bytes 196
  66.8 4.4 copy-start.33
  66.8 4.4 copy-start.35
  67.5 12.9 %copy-start.37 = (bf16[8,16]{1,0:T(8,128)(2,1)}, bf16[8,16]{1,0:T(8,128)(2,1)S(1)}, u32[]{:S(2)}) copy-start(bf16[8,16]{1,0:T(8,128)(2,1)S(1)} %get-tuple-element.92) | copy-start | bytes 772
  73.3 18.3 %copy-start.10 = (bf16[2048,512]{1,0:T(8,128)(2,1)}, bf16[2048,512]{1,0:T(8,128)(2,1)S(1)}, u32[]{:S(2)}) copy-start(bf16[2048,512]{1,0:T(8,128)(2,1)S(1)} %multiply_convert_fusion.5) | copy-start | bytes 6291460
  75.3 16.2 %copy-start.16 = (bf16[8,16,16,512]{3,2,1,0:T(8,128)(2,1)}, bf16[8,16,16,512]{3,2,1,0:T(8,128)(2,1)S(1)}, u32[]{:S(2)}) copy-start(bf16[8,16,16,512]{3,2,1,0:T(8,128)(2,1)S(1)} %get-tuple-element.78) | copy-start | bytes 6291460
  75.3 16.2 %copy-start.17 = (bf16[8,16,16,512]{3,2,1,0:T(8,128)(2,1)}, bf16[8,16,16,512]{3,2,1,0:T(8,128)(2,1)S(1)}, u32[]{:S(2)}) copy-start(bf16[8,16,16,512]{3,2,1,0:T(8,128)(2,1)S(1)} %get-tuple-element.79) | copy-start | bytes 6291460
  95.1 14.1 %copy-start.47 = (f32[512]{0:T(512)S(1)}, f32[512]{0:T(512)}, u32[]{:S(2)}) copy-start(f32[512]{0:T(512)} %param.23) | copy-start | bytes 6148
  95.1 14.8 %copy-start.53 = (f32[512]{0:T(512)S(1)}, f32[512]{0:T(512)}, u32[]{:S(2)}) copy-start(f32[512]{0:T(512)} %param.24) | copy-start | bytes 6148
  108.3 4.5 copy-start.55
  112.8 8.8 %copy-start.23 = (bf16[2048,512]{1,0:T(8,128)(2,1)}, bf16[2048,512]{1,0:T(8,128)(2,1)S(1)}, u32[]{:S(2)}) copy-start(bf16[2048,512]{1,0:T(8,128)(2,1)S(1)} %multiply_convert_fusion.4) | copy-start | bytes 6291460
  121.6 19.6 %copy-start.30 = (bf16[1,2048,256]{2,1,0:T(8,128)(2,1)S(1)}, bf16[1,2048,256]{2,1,0:T(8,128)(2,1)}, u32[]{:S(2)}) copy-start(bf16[1,2048,256]{2,1,0:T(8,128)(2,1)} %param.20) | copy-start | bytes 3145732
  141.2 12.2 %copy-start.2 = (f32[2048,2048]{1,0:T(8,128)S(1)}, f32[2048,2048]{1,0:T(8,128)}, u32[]{:S(2)}) copy-start(f32[2048,2048]{1,0:T(8,128)} %get-tuple-element.98) | copy-start | bytes 50331652
  147.9 5.5 copy-start.40
  147.9 5.5 copy-start.50
  153.4 11.7 %copy-start.41 = (f32[8,128]{1,0:T(8,128)S(1)}, f32[8,128]{1,0:T(8,128)}, u32[]{:S(2)}) copy-start(f32[8,128]{1,0:T(8,128)} %stats_0.1) | copy-start | bytes 12292
  165.1 7.8 %copy-start.32 = (f32[32,128]{1,0:T(8,128)S(1)}, f32[32,128]{1,0:T(8,128)}, u32[]{:S(2)}) copy-start(f32[32,128]{1,0:T(8,128)} %stats_2.1) | copy-start | bytes 49156
  173.0 8.9 %copy-start.13 = (f32[2048,2048]{1,0:T(8,128)S(1)}, f32[2048,2048]{1,0:T(8,128)}, u32[]{:S(2)}) copy-start(f32[2048,2048]{1,0:T(8,128)} %get-tuple-element.65) | copy-start | bytes 50331652
  222.2 12.9 %copy-start.39 = (f32[2048]{0:T(1024)}, f32[2048]{0:T(1024)S(1)}, u32[]{:S(2)}) copy-start(f32[2048]{0:T(1024)S(1)} %slice_bitcast_fusion.3) | copy-start | bytes 24580
  222.2 12.9 %copy-start.8 = (f32[2048,512]{1,0:T(8,128)S(1)}, f32[2048,512]{1,0:T(8,128)}, u32[]{:S(2)}) copy-start(f32[2048,512]{1,0:T(8,128)} %copy-done.7) | copy-start | bytes 12582916
  222.2 13.0 %copy-start.56 = (bf16[512,2048]{1,0:T(8,128)(2,1)S(1)}, bf16[512,2048]{1,0:T(8,128)(2,1)}, u32[]{:S(2)}) copy-start(bf16[512,2048]{1,0:T(8,128)(2,1)} %param.19) | copy-start | bytes 6291460
  235.1 7.8 %copy-start.14 = (bf16[2048,2048]{1,0:T(8,128)(2,1)}, bf16[2048,2048]{1,0:T(8,128)(2,1)S(1)}, u32[]{:S(2)}) copy-start(bf16[2048,2048]{1,0:T(8,128)(2,1)S(1)} %multiply_convert_fusion) | copy-start | bytes 25165828
  235.2 20.7 %copy-start.24 = (bf16[2048,512]{1,0:T(8,128)(2,1)S(1)}, bf16[2048,512]{1,0:T(8,128)(2,1)}, u32[]{:S(2)}) copy-start(bf16[2048,512]{1,0:T(8,128)(2,1)} %copy-done.23) | copy-start | bytes 6291460
  255.9 9.5 %copy-start.48 = (f32[512]{0:T(512)}, f32[512]{0:T(512)S(1)}, u32[]{:S(2)}) copy-start(f32[512]{0:T(512)S(1)} %slice_bitcast_fusion.7) | copy-start | bytes 6148
  255.9 9.5 %copy-start.9 = (f32[2048,512]{1,0:T(8,128)S(1)}, f32[2048,512]{1,0:T(8,128)}, u32[]{:S(2)}) copy-start(f32[2048,512]{1,0:T(8,128)} %copy-done.7) | copy-start | bytes 12582916
  255.9 9.5 %copy-start.18 = (f32[2048,512]{1,0:T(8,128)S(1)}, f32[2048,512]{1,0:T(8,128)}, u32[]{:S(2)}) copy-start(f32[2048,512]{1,0:T(8,128)} %get-tuple-element.100) | copy-start | bytes 12582916
  266.6 11.4 %copy-start.15 = (bf16[2048,512]{1,0:T(8,128)(2,1)}, bf16[2048,512]{1,0:T(8,128)(2,1)S(1)}, u32[]{:S(2)}) copy-start(bf16[2048,512]{1,0:T(8,128)(2,1)S(1)} %multiply_convert_fusion.3) | copy-start | bytes 6291460
  267.5 10.5 %copy-start.25 = (bf16[8,16,16,512]{3,2,1,0:T(8,128)(2,1)}, bf16[8,16,16,512]{3,2,1,0:T(8,128)(2,1)S(1)}, u32[]{:S(2)}) copy-start(bf16[8,16,16,512]{3,2,1,0:T(8,128)(2,1)S(1)} %get-tuple-element.101) | copy-start | bytes 6291460
  267.5 10.5 %copy-start.26 = (bf16[8,16,16,512]{3,2,1,0:T(8,128)(2,1)}, bf16[8,16,16,512]{3,2,1,0:T(8,128)(2,1)S(1)}, u32[]{:S(2)}) copy-start(bf16[8,16,16,512]{3,2,1,0:T(8,128)(2,1)S(1)} %get-tuple-element.102) | copy-start | bytes 6291460
  273.1 4.9 copy-start.28
  278.1 6.0 copy-start.5
  278.1 6.0 copy-start.34
  278.1 6.0 copy-start.36
  278.1 6.0 copy-start.46
  300.6 7.0 %copy-start.49 = (f32[512]{0:T(512)}, f32[512]{0:T(512)S(1)}, u32[]{:S(2)}) copy-start(f32[512]{0:T(512)S(1)} %slice_bitcast_fusion.5) | copy-start | bytes 6148
  300.6 7.0 %copy-start.6 = (f32[2048,512]{1,0:T(8,128)S(1)}, f32[2048,512]{1,0:T(8,128)}, u32[]{:S(2)}) copy-start(f32[2048,512]{1,0:T(8,128)} %copy-done.3) | copy-start | bytes 12582916
  300.6 7.0 %copy-start.12 = (f32[2048,512]{1,0:T(8,128)S(1)}, f32[2048,512]{1,0:T(8,128)}, u32[]{:S(2)}) copy-start(f32[2048,512]{1,0:T(8,128)} %get-tuple-element.59) | copy-start | bytes 12582916
  306.9 24.4 %collective-permute-start.3 = (bf16[2048,256]{1,0:T(8,128)(2,1)S(1)}, bf16[2048,256]{1,0:T(8,128)(2,1)S(1)}, u32[]{:S(2)}, u32[]{:S(2)}) collective-permute-start(bf16[2048,256]{1,0:T(8,128)(2,1)S(1)} %convolution_convert_fusion.2), channel_id=1, source_target_pairs={{0,16},{16,0},{1,17},{17,1},{2,18},{18,2},{3,19},{19,3},{4,20},{20... | collective-permute-start | bytes 3145736 | tf_op jit(solution)/shard_map/ppermute | solution.py:239
  310.2 21.1 %copy-start.22 = (f32[2048,256]{1,0:T(8,128)S(1)}, f32[2048,256]{1,0:T(8,128)}, u32[]{:S(2)}) copy-start(f32[2048,256]{1,0:T(8,128)} %fusion.37) | copy-start | bytes 6291460
  319.4 13.3 %copy-start.11 = (bf16[2048,512]{1,0:T(8,128)(2,1)S(1)}, bf16[2048,512]{1,0:T(8,128)(2,1)}, u32[]{:S(2)}) copy-start(bf16[2048,512]{1,0:T(8,128)(2,1)} %copy-done.10) | copy-start | bytes 6291460
  332.7 284.4 %all-reduce.14.cloned.1.call-start = ((), (), s32[]{:S(2)}) async-start(), calls=%async_computation.1 | async-start | bytes 17825792 | tf_op jit(solution)/shard_map/psum | solution.py:286
  373.4 7.8 %copy-start.20 = (bf16[2048,512]{1,0:T(8,128)(2,1)S(1)}, bf16[2048,512]{1,0:T(8,128)(2,1)}, u32[]{:S(2)}) copy-start(bf16[2048,512]{1,0:T(8,128)(2,1)} %copy-done.19) | copy-start | bytes 6291460
  380.6 23.7 %collective-permute-start.1 = (bf16[2048,256]{1,0:T(8,128)(2,1)}, bf16[2048,256]{1,0:T(8,128)(2,1)}, u32[]{:S(2)}, u32[]{:S(2)}) collective-permute-start(bf16[2048,256]{1,0:T(8,128)(2,1)} %convolution_convert_fusion.3), channel_id=1, source_target_pairs={{0,16},{16,0},{1,17},{17,1},{2,18},{18,2},{3,19},{19,3},{4,20},{20... | collective-permute-start | bytes 3145736 | tf_op jit(solution)/shard_map/ppermute | solution.py:232
  617.1 7.5 %copy-start.21 = (bf16[512,2048]{1,0:T(8,128)(2,1)S(1)}, bf16[512,2048]{1,0:T(8,128)(2,1)}, u32[]{:S(2)}) copy-start(bf16[512,2048]{1,0:T(8,128)(2,1)} %get-tuple-element.56) | copy-start | bytes 6291460
  624.6 6.7 %copy-start.1 = (bf16[1,2,8,256,256]{4,3,2,1,0:T(8,128)(2,1)S(1)}, bf16[1,2,8,256,256]{4,3,2,1,0:T(8,128)(2,1)}, u32[]{:S(2)}) copy-start(bf16[1,2,8,256,256]{4,3,2,1,0:T(8,128)(2,1)} %param.27) | copy-start | bytes 6291460
  (15 other events, 37.9 us)
Sparse Core Ops, SparseCore 0:
  332.8 92.4 all-reduce.11
  432.0 184.9 all-reduce.13

commit v2 on v1

--- a/solution.py
+++ b/solution.py
@@ -1,4 +1,5 @@
 import functools
+import math
 
 import jax
 import jax.numpy as jnp
@@ -136,6 +137,300 @@
     return out[:half].reshape(width), out[half:].reshape(width)
 
 
+class Reduction:
+    def __init__(self, grid, work, result, room, send, recv, far_send, far_recv, wide):
+        self.grid, self.work, self.result, self.room = grid, work, result, room
+        self.send, self.recv, self.far_send, self.far_recv = send, recv, far_send, far_recv
+        self.wide = wide
+        self.rows, self.cols = work.shape
+        sizes = self.sizes(self.rows, self.cols, wide, grid.far)
+        self.flat = sizes[3] == sizes[2] and grid.far > 1
+        self.copies = {}
+
+    @staticmethod
+    def sizes(rows, cols, wide, far):
+        if wide:
+            core = (rows, cols // 2)
+            first = (rows, cols // 8)
+            second = (rows, cols // 16)
+        else:
+            core = (rows // 2, cols)
+            first = (rows // 2, cols // 4)
+            second = (rows // 4, cols // 4)
+        if second[0] % (8 * far):
+            return core, first, second, second
+        return core, first, second, (second[0] // far, second[1])
+
+    @staticmethod
+    def room_shapes(rows, cols, wide, far):
+        core, first, second, last = Reduction.sizes(rows, cols, wide, far)
+        return [
+            pltpu.VMEM(core, jnp.bfloat16),
+            pltpu.VMEM((2,) + first, jnp.bfloat16),
+            pltpu.VMEM((2,) + second, jnp.bfloat16),
+            pltpu.VMEM((2, far) + last, jnp.bfloat16),
+            pltpu.SemaphoreType.DMA((10,)),
+            pltpu.SemaphoreType.DMA((10,)),
+            pltpu.SemaphoreType.DMA((4, far)),
+            pltpu.SemaphoreType.DMA((4, far)),
+        ]
+
+    def view(self, core, part=None, first=None, second=None, piece=None, done=False):
+        grid = self.grid
+        sizes = self.sizes(self.rows, self.cols, self.wide, grid.far)
+        row = col = 0
+        if self.wide:
+            col = core * (self.cols // 2)
+            shape = sizes[0]
+            if part is not None:
+                col = col + part * (self.cols // 4) + first * (self.cols // 8)
+                shape = sizes[1]
+            if second is not None:
+                col = col + second * (self.cols // 16)
+                shape = sizes[2]
+        else:
+            row = core * (self.rows // 2)
+            shape = sizes[0]
+            if part is not None:
+                col = part * (self.cols // 2) + first * (self.cols // 4)
+                shape = sizes[1]
+            if second is not None:
+                row = row + second * (self.rows // 4)
+                shape = sizes[2]
+        if piece is not None and not self.flat:
+            row = row + piece * sizes[3][0]
+            shape = sizes[3]
+        if not isinstance(row, int):
+            row = pl.multiple_of(row, shape[0] & -shape[0])
+        if not isinstance(col, int):
+            col = pl.multiple_of(col, 128)
+        ref = self.result if done else self.work
+        return ref.at[pl.ds(row, shape[0]), pl.ds(col, shape[1])]
+
+    def swap(self, index, source, target, device):
+        copy = pltpu.make_async_remote_copy(
+            src_ref=source,
+            dst_ref=target,
+            send_sem=self.send.at[index],
+            recv_sem=self.recv.at[index],
+            device_id=device,
+            device_id_type=MESH,
+        )
+        copy.start()
+        self.copies[index] = copy
+
+    def settle(self, *indices):
+        for index in indices:
+            self.copies.pop(index).wait()
+
+    def add(self, target, sources):
+        rows = target.shape[0]
+        step = math.gcd(rows, 64)
+
+        def one(i, carry):
+            span = pl.ds(pl.multiple_of(i * step, step), step)
+            total = sources[0][span].astype(jnp.float32)
+            for source in sources[1:]:
+                total = total + source[span].astype(jnp.float32)
+            target[span] = total.astype(jnp.bfloat16)
+            return carry
+
+        lax.fori_loop(0, rows // step, one, 0)
+
+    def join(self, mine, received):
+        self.add(mine, [mine, received])
+
+    def far_copy(self, part, step, back, inward):
+        grid = self.grid
+        bits = grid.bits(part)
+        slot = lax.rem(grid.high + step, grid.far)
+        owner = slot if inward else grid.high
+        if back:
+            source = self.view(grid.core, part, bits[0], bits[1], grid.high, True)
+            target = self.view(grid.core, part, bits[0], bits[1], owner, True)
+        else:
+            source = self.view(grid.core, part, bits[0], bits[1], slot)
+            target = self.room[3].at[part, owner]
+        line = 2 * part + (1 if back else 0)
+        return pltpu.make_async_remote_copy(
+            src_ref=source,
+            dst_ref=target,
+            send_sem=self.far_send.at[line, step],
+            recv_sem=self.far_recv.at[line, owner],
+            device_id=(grid.task, slot * LOW + grid.low),
+            device_id_type=MESH,
+        )
+
+    def far_start(self, back):
+        for part in range(2):
+            for step in range(1, self.grid.far):
+                self.far_copy(part, step, back, False).start()
+
+    def far_settle(self, back):
+        for part in range(2):
+            for step in range(1, self.grid.far):
+                self.far_copy(part, step, back, True).wait_recv()
+                self.far_copy(part, step, back, False).wait_send()
+
+    def stage(self, index):
+        grid = self.grid
+        other = 1 - grid.core
+        if index == 0:
+            self.swap(0, self.view(other), self.room[0], grid.core_peer)
+        elif index == 1:
+            self.settle(0)
+            self.join(self.view(grid.core), self.room[0])
+            for part in range(2):
+                bit = grid.bits(part)[0]
+                self.swap(1 + part, self.view(grid.core, part, 1 - bit), self.room[1].at[part], grid.peers(part)[0])
+        elif index == 2:
+            self.settle(1, 2)
+            for part in range(2):
+                bits = grid.bits(part)
+                self.join(self.view(grid.core, part, bits[0]), self.room[1].at[part])
+                self.swap(
+                    3 + part,
+                    self.view(grid.core, part, bits[0], 1 - bits[1]),
+                    self.room[2].at[part],
+                    grid.peers(part)[1],
+                )
+        elif index == 3:
+            self.settle(3, 4)
+            for part in range(2):
+                bits = grid.bits(part)
+                self.join(self.view(grid.core, part, bits[0], bits[1]), self.room[2].at[part])
+            self.far_start(False)
+        elif index == 4:
+            self.far_settle(False)
+            for part in range(2):
+                bits = grid.bits(part)
+                mine = self.view(grid.core, part, bits[0], bits[1], grid.high)
+                self.room[3][part, grid.high] = mine[...]
+                self.add(
+                    self.view(grid.core, part, bits[0], bits[1], grid.high, True),
+                    [self.room[3].at[part, slot] for slot in range(grid.far)],
+                )
+            if not self.flat:
+                self.far_start(True)
+        elif index == 5:
+            if not self.flat:
+                self.far_settle(True)
+            for part in range(2):
+                bits = grid.bits(part)
+                mine = self.view(grid.core, part, bits[0], bits[1], done=True)
+                self.swap(5 + part, mine, mine, grid.peers(part)[1])
+        elif index == 6:
+            self.settle(5, 6)
+            for part in range(2):
+                mine = self.view(grid.core, part, grid.bits(part)[0], done=True)
+                self.swap(7 + part, mine, mine, grid.peers(part)[0])
+        elif index == 7:
+            self.settle(7, 8)
+            mine = self.view(grid.core, done=True)
+            self.swap(9, mine, mine, grid.core_peer)
+        elif index == 8:
+            self.settle(9)
+
+
+class Grid:
+    def __init__(self, batch):
+        self.task = lax.axis_index("task")
+        place = lax.axis_index("batch")
+        self.far = batch // LOW
+        self.high = place // LOW
+        self.low = lax.rem(place, LOW)
+        self.core = lax.rem(place, 2)
+        self.y = lax.rem(place // 2, 2)
+        base = place - self.low
+        self.core_peer = (self.task, base + self.y * 2 + (1 - self.core))
+        self.x_peer = (1 - self.task, place)
+        self.y_peer = (self.task, base + (1 - self.y) * 2 + self.core)
+
+    def bits(self, part):
+        return (self.task, self.y) if part == 0 else (self.y, self.task)
+
+    def peers(self, part):
+        return (self.x_peer, self.y_peer) if part == 0 else (self.y_peer, self.x_peer)
+
+    def far_peers(self):
+        return [
+            (self.task, lax.rem(self.high + step, self.far) * LOW + self.low) for step in range(1, self.far)
+        ]
+
+    def meet(self):
+        barrier = pltpu.get_barrier_semaphore()
+        everyone = [self.core_peer, self.x_peer, self.y_peer] + self.far_peers()
+        for device in everyone:
+            pl.semaphore_signal(barrier, inc=1, device_id=device, device_id_type=MESH)
+        return lambda: pl.semaphore_wait(barrier, len(everyone))
+
+
+def sum_kernel(shapes, batch, *refs):
+    count = len(shapes)
+    sources, results = refs[:count], refs[count : 2 * count]
+    refs = refs[2 * count :]
+    works, refs = refs[:count], refs[count:]
+    totals, refs = refs[:count], refs[count:]
+    local, refs = refs[0], refs[1:]
+    grid = Grid(batch)
+    wait = grid.meet()
+    chunks = []
+    loads = []
+    number = 0
+    for item, (rows, cols, pieces, wide) in enumerate(shapes):
+        width = cols // pieces
+        for piece in range(pieces):
+            span = pl.ds(piece * width, width)
+            load = pltpu.make_async_copy(
+                sources[item].at[:, span], works[item].at[:, span], local.at[number]
+            )
+            load.start()
+            store = pltpu.make_async_copy(
+                totals[item].at[:, span], results[item].at[:, span], local.at[number]
+            )
+            loads.append((load, store))
+            room = refs[8 * number : 8 * number + 8]
+            chunks.append(
+                Reduction(grid, works[item].at[:, span], totals[item].at[:, span], room[:4], room[4], room[5], room[6], room[7], wide)
+            )
+            number += 1
+    wait()
+    for wave in range(number + 8):
+        for stage in range(8, -1, -1):
+            chunk = wave - stage
+            if 0 <= chunk < number:
+                if stage == 0:
+                    loads[chunk][0].wait()
+                chunks[chunk].stage(stage)
+                if stage == 8:
+                    loads[chunk][1].start()
+    for load, store in loads:
+        store.wait()
+
+
+def sum_all(arrays, pieces, wides, ident):
+    batch = lax.axis_size("batch")
+    far = batch // LOW
+    shapes = [a.shape + (p, w) for a, p, w in zip(arrays, pieces, wides)]
+    rooms = []
+    for rows, cols, piece, wide in shapes:
+        for _ in range(piece):
+            rooms += Reduction.room_shapes(rows, cols // piece, wide, far)
+    return pl.pallas_call(
+        functools.partial(sum_kernel, shapes, batch),
+        out_shape=[jax.ShapeDtypeStruct(a.shape, jnp.bfloat16) for a in arrays],
+        in_specs=[pl.BlockSpec(memory_space=pl.ANY)] * len(arrays),
+        out_specs=[pl.BlockSpec(memory_space=pl.ANY)] * len(arrays),
+        scratch_shapes=[pltpu.VMEM(a.shape, jnp.bfloat16) for a in arrays + arrays]
+        + [pltpu.SemaphoreType.DMA((sum(pieces),))]
+        + rooms,
+        compiler_params=pltpu.CompilerParams(
+            collective_id=ident, has_side_effects=True, vmem_limit_bytes=56 * 2**20
+        ),
+        name="sum_all",
+    )(*arrays)
+
+
 def norm_forward(hidden, gain, bias, ident):
     rows = hidden.shape[0]
     count = lax.axis_size("task") * lax.axis_size("batch") * rows
@@ -188,13 +483,6 @@
     out_width = w_heads.shape[2]
     task = lax.axis_index("task")
     swap = [(0, 1), (1, 0)]
-    cot = cotangent.reshape(2, rows, out_width)
-    cot_mine = lax.dynamic_index_in_dim(cot, task, 0, keepdims=False)
-    cot_send = lax.dynamic_index_in_dim(cot, 1 - task, 0, keepdims=False)
-    cot_peer = lax.ppermute(cot_send, "task", swap)
-    heads_mine = w_heads[0]
-    heads_peer = lax.ppermute(heads_mine, "task", swap)
-
     lines = jnp.arange(SIDE, dtype=jnp.int32)
     cuts = crop_cuts.reshape(canvases, 2)
     row_edge = lines[None, :] == cuts[:, 0:1]
@@ -209,6 +497,11 @@
     flat_in = inputs.reshape(rows, width)
     h_one = jnp.dot(flat_in, w_reduce, preferred_element_type=full)
     n_one, xh_one, inv_one = norm_forward(h_one, gain_one, bias_one, 0)
+    cot = cotangent.reshape(2, rows, out_width)
+    cot_mine = lax.dynamic_index_in_dim(cot, task, 0, keepdims=False)
+    cot_send = lax.dynamic_index_in_dim(cot, 1 - task, 0, keepdims=False)
+    cot_send, inv_one = lax.optimization_barrier((cot_send, inv_one))
+    cot_peer = lax.ppermute(cot_send, "task", swap)
     q_one = (n_one * bulk(n_one)).astype(low).reshape(canvases, SIDE, SIDE, mid)
     sides = jnp.concatenate(
         [moved(q_one, 0, -1) * by_col(from_left), q_one, moved(q_one, 0, 1) * by_col(from_right)],
@@ -221,23 +514,26 @@
         + jnp.dot((moved(sides, 1, 0) * by_row(from_below)).reshape(rows, -1), taps[2], preferred_element_type=full)
     )
     n_two, xh_two, inv_two = norm_forward(h_two, gain_two, bias_two, 1)
+    heads_mine = w_heads[0]
+    heads_sent, inv_two = lax.optimization_barrier((heads_mine, inv_two))
+    heads_peer = lax.ppermute(heads_sent, "task", swap)
     q_two = (n_two * bulk(n_two)).astype(low)
     h_three = jnp.dot(q_two, w_expand, preferred_element_type=full)
     n_three, xh_three, inv_three = norm_forward(h_three, gain_three, bias_three, 2)
     before = n_three + flat_in.astype(full)
     trunk = (before * bulk(before)).astype(low)
 
+    first_task = task == 0
+    cots = [jnp.where(first_task, cot_mine, cot_peer), jnp.where(first_task, cot_peer, cot_mine)]
+    tops = [jnp.where(first_task, heads_mine, heads_peer), jnp.where(first_task, heads_peer, heads_mine)]
+    cot_both = jnp.concatenate(cots, axis=1)
     out_mine = jnp.dot(trunk, heads_mine, preferred_element_type=full)
     out_sent = jnp.dot(trunk, heads_peer, preferred_element_type=full).astype(low)
     out_peer = lax.ppermute(out_sent, "task", swap).astype(full)
-    first = jnp.where(task == 0, out_mine, out_peer)
-    second = jnp.where(task == 0, out_peer, out_mine)
+    first = jnp.where(first_task, out_mine, out_peer)
+    second = jnp.where(first_task, out_peer, out_mine)
     head_out = jnp.stack([first, second]).reshape(1, 2, canvases, pixels, out_width)
-
-    grad_mine = lax.dot_general(trunk, cot_mine, ROWS_ROWS, preferred_element_type=full)
-    grad_sent = lax.dot_general(trunk, cot_peer, ROWS_ROWS, preferred_element_type=full)
-    grad_other = lax.ppermute(grad_sent.astype(low), "task", swap).astype(full)
-    grad_heads = lax.psum((grad_mine + grad_other).astype(low), "batch").astype(full)[None]
+    grad_heads = lax.dot_general(trunk, cot_both, ROWS_ROWS, preferred_element_type=full)
 
     g_mine = lax.dot_general(cot_mine, heads_mine, COLS_COLS, preferred_element_type=full)
     g_peer = lax.dot_general(cot_peer, heads_peer, COLS_COLS, preferred_element_type=full)
@@ -252,7 +548,6 @@
     flow = merged * slope(before)
     dh_three, dg_three, db_three = norm_backward(flow, xh_three, inv_three, gain_three, 3)
     grad_expand = lax.dot_general(q_two, dh_three, ROWS_ROWS, preferred_element_type=full)
-    grad_expand = lax.psum(grad_expand.astype(low), ("task", "batch")).astype(full)
     dq_two = lax.dot_general(dh_three, w_expand, COLS_COLS, preferred_element_type=full)
     dh_two, dg_two, db_two = norm_backward(dq_two * slope(n_two), xh_two, inv_two, gain_two, 4)
     up = dh_two.reshape(canvases, SIDE, SIDE, mid)
@@ -278,12 +573,19 @@
     grad_spatial = lax.dot_general(
         sides.reshape(rows, 3 * mid), lanes, ROWS_ROWS, preferred_element_type=full
     )
-    grad_spatial = lax.psum(grad_spatial.astype(low), ("task", "batch"))
+    grad_reduce = lax.dot_general(flat_in, dh_one, ROWS_ROWS, preferred_element_type=full)
+    grad_heads, grad_expand, grad_spatial, grad_reduce = sum_all(
+        [g.astype(low) for g in (grad_heads, grad_expand, grad_spatial, grad_reduce)],
+        [1, 1, 3, 1],
+        [False, True, False, False],
+        6,
+    )
     grad_spatial = (
         grad_spatial.reshape(3, mid, 3, mid).transpose(2, 0, 1, 3).reshape(w_spatial.shape).astype(full)
     )
-    grad_reduce = lax.dot_general(flat_in, dh_one, ROWS_ROWS, preferred_element_type=full)
-    grad_reduce = lax.psum(grad_reduce.astype(low), ("task", "batch")).astype(full)
+    grad_heads = lax.dynamic_slice_in_dim(grad_heads, task * out_width, out_width, axis=1).astype(full)[None]
+    grad_expand = grad_expand.astype(full)
+    grad_reduce = grad_reduce.astype(full)
     grad_inputs = (
         flow + lax.dot_general(dh_one, w_reduce, COLS_COLS, preferred_element_type=full)
     ).astype(low)

time: 645 us -> 515 us (0.80)
  waiting for transfers between devices: 230 us -> 13.1 us
  Pallas kernels: 94 us -> 191 us
  between operations: 15 us -> 1.59 us
    psum x2 -> x0, waiting for transfers between devices: 206 us -> none  [the longest x1 189 us: body(): lax.psum(grad_reduce.astype(low), ('task', 'batch')).astype(full)]
    pallas_call x0 -> x1, Pallas kernels: none -> 108 us  [sum_all(): pl.pallas_call(functools.partial(sum_kernel, shapes, batch), out_shape=[j...]
    ppermute x2 -> x1, waiting for transfers between devices: 11.9 us -> 0.01 us  [body(): heads_peer = lax.ppermute(heads_sent, 'task', swap)]
    pallas_call x6, Pallas kernels: 94 us -> 83.3 us  [reduce_stats(): pl.pallas_call(functools.partial(stats_kernel, rows, forward, tasks, batc...]
    unnamed x115 -> x114, local copies, waits for them, and re-layouts: 16.6 us -> 5.95 us
    convert_element_type x2, local copies, waits for them, and re-layouts: 18 us -> 27 us  [body(): grad_spatial.reshape(3, mid, 3, mid).transpose(2, 0, 1, 3)]
    dot_general x2 -> x1, matrix products: 13.7 us -> 6.49 us  [body(): lax.dot_general(trunk, cot_both, ROWS_ROWS, preferred_element_type=full)]
  transfers between devices with their start and end apart: 6 -> 3, of which waited for: 4 -> 1; matrix products, arithmetic and copies ran while one was open for 27% -> 15% of each run, Pallas kernels for 10% -> 6%
where the time goes in v2:
time: 515 us; the launch traced here: 508 us
  Pallas kernels  191 us (37%)
  matrix products  159 us (31%)
  other arithmetic  88.1 us (17%)
  local copies, waits for them, and re-layouts  53.1 us (10%)
  waiting for transfers between devices  13.1 us (3%)
    pallas_call x1, Pallas kernels, sum_all(): pl.pallas_call(functools.partial(sum_kernel, shapes, batch), out_shape=[j...  108 us
    pallas_call x6, Pallas kernels, reduce_stats(): pl.pallas_call(functools.partial(stats_kernel, rows, forward, tasks, batc...  83.3 us
    dot_general x1, matrix products, body(): lax.dot_general(cot_peer, heads_peer, COLS_COLS, preferred_element_type=f...  28.7 us
    convert_element_type x2, local copies, waits for them, and re-layouts, body(): grad_spatial.reshape(3, mid, 3, mid).transpose(2, 0, 1, 3)  27 us
    dot_general x3, matrix products, body(): lax.dot_general(lanes, across[:, b].transpose(1, 0, 2).reshape(mid, 3 * m...  19 us
    convert_element_type x3, other arithmetic, norm_backward(): return (hidden_grad.astype(jnp.bfloat16), gain_grad, bias_grad)  18.3 us
    convert_element_type x1, other arithmetic, body(): trunk = (before * bulk(before)).astype(low)  18.1 us
    dot_general x1, matrix products, body(): lax.dot_general(sides.reshape(rows, 3 * mid), lanes, ROWS_ROWS, preferred...  15.4 us
  transfers between devices with their start and end apart: 3, of which 1 were waited for; matrix products, arithmetic and copies ran while one was open for 15% of the time, Pallas kernels for 6%

profile of v2, /device:TPU:0, one launch (start us, length us, event | category | flops | bytes accessed | tf_op | source)
XLA Modules:
  0.0 508.4 jit_solution(13295406440249867255)
XLA Ops:
  0.7 7.7 %fusion.61 = (f32[512]{0:T(512)S(1)}, f32[2048,512]{1,0:T(8,128)S(1)}) fusion(bf16[2048,2048]{1,0:T(8,128)(2,1)} %bitcast.152, bf16[2048,512]{1,0:T(8,128)(2,1)} %param.17), kind=kOutput, calls=%fused_computation.147 | convolution fusion | flops 4296015360 | bytes 14682112 | tf_op jit(solution)/shard_map/dot_general | solution.py:498
  8.4 2.0 copy-done.2
  11.5 12.9 %stats_0.1 = f32[8,128]{1,0:T(8,128)} custom-call(f32[8,128]{1,0:T(8,128)} %pad_maximum_fusion.5.local), custom_call_target="tpu_custom_call" | custom-call | tf_op jit(solution)/shard_map/stats_0/pallas_call | solution.py:119
  26.6 2.9 fusion.60
  31.6 2.0 fusion.34
  33.6 5.0 pad_maximum_fusion
  38.7 4.1 fusion.11
  42.8 3.4 fusion.64
  46.3 3.4 fusion.65
  49.7 3.5 fusion.62
  56.4 10.9 %stats_1.1 = f32[8,128]{1,0:T(8,128)} custom-call(f32[8,128]{1,0:T(8,128)} %pad_maximum_fusion.6.local), custom_call_target="tpu_custom_call" | custom-call | tf_op jit(solution)/shard_map/stats_1/pallas_call | solution.py:119
  68.7 2.3 dynamic-slice_bitcast_fusion
  72.4 2.9 multiply_convert_fusion.4
  75.3 8.5 %fusion.63 = (f32[2048]{0:T(1024)S(1)}, f32[2048,2048]{1,0:T(8,128)}) fusion(bf16[2048,512]{1,0:T(8,128)(2,1)S(1)} %multiply_convert_fusion.4, bf16[512,2048]{1,0:T(8,128)(2,1)S(1)} %copy-done), kind=kOutput, calls=%fused_computation.149 | convolution fusion | flops 4299159552 | bytes 20979712 | tf_op jit(solution)/shard_map/dot_general | solution.py:521
  83.9 7.5 %multiply_reduce_fusion.1 = f32[2048]{0:T(1024)S(1)} fusion(f32[2048,2048]{1,0:T(8,128)} %get-tuple-element.77, f32[2048]{0:T(1024)S(1)} %broadcast_multiply_fusion.3), kind=kLoop, calls=%fused_computation.23 | loop fusion | flops 12580864 | bytes 16793600 | tf_op jit(solution)/shard_map/reduce_sum | solution.py:438
  92.0 29.0 %stats_2.1 = f32[32,128]{1,0:T(8,128)} custom-call(f32[32,128]{1,0:T(8,128)} %pad_maximum_fusion.3.local), custom_call_target="tpu_custom_call" | custom-call | tf_op jit(solution)/shard_map/stats_2/pallas_call | solution.py:119
  121.7 7.1 %fusion.39 = bf16[2048,2048]{1,0:T(8,128)(2,1)} fusion(bf16[2,2048,256]{2,1,0:T(8,128)(2,1)} %bitcast.163, s32[]{:T(128)S(6)} %select_n.35, bf16[1,2048,256]{2,1,0:T(8,128)(2,1)S(1)} %copy-done.27), kind=kOutput, calls=%fused_computation.93 | convolution fusion | flops 2147483648 | bytes 10485764 | tf_op jit(solution)/shard_map/dot_general | solution.py:538
  128.7 18.1 %multiply_convert_fusion.1 = (bf16[2048,2048]{1,0:T(8,128)(2,1)}, f32[2048,2048]{1,0:T(8,128)}) fusion(bf16[1,8,256,2048]{3,2,1,0:T(8,128)(2,1)} %param.14, f32[2048]{0:T(1024)S(1)} %copy-done.48, f32[2048]{0:T(1024)S(1)} %copy-done.37, f32[2048]{0:T(1024)S(1)} %get-tuple-element.60, f32[2048,2048]{1,0:T(8,128)} %get-tuple-element.77, ...), kind=kLoop, calls=%fused_computation.19 | loop fusion | flops 46137344 | bytes 50364416 | tf_op jit(solution)/shard_map/convert_element_type | solution.py:524
  146.9 2.3 slice_bitcast_fusion.2
  149.2 2.6 copy.39
  151.7 2.6 copy.37
  154.4 2.6 copy.35
  157.5 7.1 %fusion.52 = f32[2048,256]{1,0:T(8,128)} fusion(bf16[2048,2048]{1,0:T(8,128)(2,1)} %get-tuple-element.41, bf16[1,2048,256]{2,1,0:T(8,128)(2,1)S(1)} %copy-done.27), kind=kOutput, calls=%fused_computation.138 | convolution fusion | flops 2147483648 | bytes 11534336 | tf_op jit(solution)/shard_map/dot_general | solution.py:530
  164.6 28.7 %fusion.56 = (f32[2048]{0:T(1024)S(1)}, f32[2048]{0:T(1024)S(1)}, f32[2048,2048]{1,0:T(8,128)}) fusion(f32[2048]{0:T(1024)S(1)} %get-tuple-element.60, f32[2048,2048]{1,0:T(8,128)} %get-tuple-element.77, f32[2048]{0:T(1024)S(1)} %get-tuple-element.59, f32[2048,2048]{1,0:T(8,128)} %get-tuple-element.42, bf16[1,8,256,2048]{3,2,1,0:T(8,128)(2,1)} %param.16, ...), kind=kOutput, calls=%fused_computation.143 | convolution fusion | flops 2290085888 | bytes 69238784 | tf_op jit(solution)/shard_map/dot_general | solution.py:539
  193.9 10.6 %stats_3.1 = f32[32,128]{1,0:T(8,128)} custom-call(f32[32,128]{1,0:T(8,128)} %pad_maximum_fusion.4.local), custom_call_target="tpu_custom_call" | custom-call | tf_op jit(solution)/shard_map/stats_3/pallas_call | solution.py:119
  206.5 12.3 %multiply_convert_fusion = bf16[2048,2048]{1,0:T(8,128)(2,1)S(1)} fusion(f32[2048,2048]{1,0:T(8,128)} %get-tuple-element.78, f32[2048,2048]{1,0:T(8,128)} %get-tuple-element.77, f32[2048]{0:T(1024)S(1)} %slice_bitcast_fusion.3, f32[2048]{0:T(1024)S(1)} %get-tuple-element.39, f32[2048]{0:T(1024)S(1)} %fusion.55, f32[2048]{0:T(1024)S(1)} %get-tuple-element.60, ...), kind=kLoop, calls=%fused_computation.17 | loop fusion | flops 33554432 | bytes 41984000 | tf_op jit(solution)/shard_map/convert_element_type | solution.py:453
  218.9 8.0 %fusion.58 = (f32[512]{0:T(512)S(1)}, f32[512]{0:T(512)S(1)}, f32[2048,512]{1,0:T(8,128)}) fusion(f32[512]{0:T(512)S(1)} %get-tuple-element.23, f32[2048,512]{1,0:T(8,128)S(1)} %copy-done.6, f32[512]{0:T(512)S(1)} %get-tuple-element.61, f32[512]{0:T(512)S(1)} %copy-done.51, f32[512]{0:T(512)S(1)} %copy-done.44, ...), kind=kOutput, calls=%fused_computation.145 | convolution fusion | flops 4311743488 | bytes 18886656 | tf_op jit(solution)/shard_map/dot_general | solution.py:551
  227.4 10.1 %stats_4.1 = f32[8,128]{1,0:T(8,128)} custom-call(f32[8,128]{1,0:T(8,128)} %pad_maximum_fusion.7.local), custom_call_target="tpu_custom_call" | custom-call | tf_op jit(solution)/shard_map/stats_4/pallas_call | solution.py:119
  239.4 10.1 %convolution_convert_fusion.1.refs_1_ = bf16[512,2048]{1,0:T(8,128)(2,1)} fusion(bf16[2048,512]{1,0:T(8,128)(2,1)} %copy-done.20, bf16[2048,2048]{1,0:T(8,128)(2,1)} %copy-done.10), kind=kOutput, calls=%fused_computation.74 | convolution fusion | flops 4296015872 | bytes 12582912 | tf_op jit(solution)/shard_map/dot_general | solution.py:550
  251.1 2.6 pad_slice_fusion.6
  254.9 15.4 %bitcast_convert_fusion.refs_2_ = bf16[1536,1536]{1,0:T(8,128)(2,1)} fusion(bf16[8,16,16,512]{3,2,1,0:T(8,128)(2,1)} %copy-done.13, bf16[8,16,16,512]{3,2,1,0:T(8,128)(2,1)S(1)} %bitcast.145, bf16[8,16,16,512]{3,2,1,0:T(8,128)(2,1)S(1)} %copy-done.12, bf16[8,16,16,512]{3,2,1,0:T(8,128)(2,1)} %get-tuple-element.80, ...), kind=kOutput, calls=%fused_computation.26 | convolution fusion | flops 9703784448 | bytes 17301504 | tf_op jit(solution)/shard_map/dot_general | solution.py:573
  270.3 7.8 %convolution_multiply_fusion = f32[8,16,16,512]{3,2,1,0:T(8,128)} fusion(bf16[512,1536,1,1]{0,1,3,2:T(8,128)(2,1)S(1)} %bitcast.170, f32[8,16]{1,0:T(8,128)S(1)} %copy-done.50, bf16[8,16,16,512]{3,2,1,0:T(8,128)(2,1)} %get-tuple-element.80, bf16[8,16,16,512]{3,2,1,0:T(8,128)(2,1)S(1)} %bitcast.149, bf16[8,16,16,512]{3,2,1,0:T(8,128)(2,1)} %get-tuple-element.81), kind=kOutput, calls=%fused_computation.80 | convolution fusion | flops 3241148416 | bytes 12059136 | tf_op jit(solution)/shard_map/dot_general | solution.py:559
  278.2 4.9 convolution_multiply_fusion.1
  283.1 6.3 %fusion.30 = f32[8,16,16,512]{3,2,1,0:T(8,128)S(1)} fusion(f32[8,16,16,512]{3,2,1,0:T(8,128)} %convolution_multiply_fusion.1, f32[8,16,16,512]{3,2,1,0:T(8,128)} %convolution_multiply_fusion, bf16[512,1536,1,1]{0,1,3,2:T(8,128)(2,1)S(1)} %bitcast.169, bf16[8,16,16,512]{3,2,1,0:T(8,128)(2,1)S(1)} %copy-done.22, bf16[8,16,16,512]{3,2,1,0:T(8,128)(2,1)S(1)} %bitcast.151, ...), kind=kOutput, calls=%fused_computation.52 | convolution fusion | flops 3242196992 | bytes 20447232 | tf_op jit(solution)/shard_map/dot_general | solution.py:559
  289.5 4.0 fusion.57
  294.0 10.0 %stats_5.1 = f32[8,128]{1,0:T(8,128)} custom-call(f32[8,128]{1,0:T(8,128)} %pad_maximum_fusion.8.local), custom_call_target="tpu_custom_call" | custom-call | tf_op jit(solution)/shard_map/stats_5/pallas_call | solution.py:119
  305.9 4.8 multiply_convert_fusion.2
  310.8 12.6 %fusion.33.refs_3_ = bf16[2048,512]{1,0:T(8,128)(2,1)} fusion(bf16[2048,512]{1,0:T(8,128)(2,1)S(1)} %multiply_convert_fusion.2, bf16[2048,2048]{1,0:T(8,128)(2,1)} %bitcast.153), kind=kOutput, calls=%fused_computation.76 | convolution fusion | flops 4296015872 | bytes 12582912 | tf_op jit(solution)/shard_map/dot_general | solution.py:576
  324.8 6.5 %convolution_convert_fusion.2.refs_0_ = bf16[2048,512]{1,0:T(8,128)(2,1)} fusion(bf16[2048,2048]{1,0:T(8,128)(2,1)S(1)} %bitcast.155, bf16[2048,256]{1,0:T(8,128)(2,1)S(1)} %get-tuple-element.52, bf16[2048,256]{1,0:T(8,128)(2,1)S(1)} %get-tuple-element.51), kind=kOutput, calls=%fused_computation.75 | convolution fusion | flops 4300210176 | bytes 12582912 | tf_op jit(solution)/shard_map/dot_general | solution.py:536
  331.3 107.9 %sum_all.1 = (bf16[2048,512]{1,0:T(8,128)(2,1)}, bf16[512,2048]{1,0:T(8,128)(2,1)}, bf16[1536,1536]{1,0:T(8,128)(2,1)}, bf16[2048,512]{1,0:T(8,128)(2,1)}) custom-call(bf16[2048,512]{1,0:T(8,128)(2,1)} %convolution_convert_fusion.2.refs_0_, bf16[512,2048]{1,0:T(8,128)(2,1)} %convolution_convert_fusion.1.refs_1_, ...), custom_call_target="tpu_custom_call" | custom-call | tf_op jit(solution)/shard_map/sum_all/pallas_call | solution.py:419
  439.2 15.5 %reshape.407 = f32[3,512,3,512]{3,2,1,0:T(4,128)} reshape(bf16[1536,1536]{1,0:T(8,128)(2,1)} %get-tuple-element.25) | data formatting | bytes 14155776 | tf_op jit(solution)/shard_map/convert_element_type | solution.py:584
  454.7 11.5 %copy.42 = f32[3,3,512,512]{3,2,1,0:T(8,128)} copy(f32[3,3,512,512]{3,0,2,1:T(4,128)} %bitcast.139) | data formatting | bytes 18874368 | tf_op jit(solution)/shard_map/convert_element_type | solution.py:584
  466.2 2.6 convert_element_type.149
  468.8 2.5 convert_element_type.154
  471.4 7.1 %convolution_convert_fusion.3 = bf16[2048,256]{1,0:T(8,128)(2,1)} fusion(bf16[2048,2048]{1,0:T(8,128)(2,1)} %get-tuple-element.41, bf16[2048,256]{1,0:T(8,128)(2,1)} %collective-permute-done), kind=kOutput, calls=%fused_computation.79 | convolution fusion | flops 2148007936 | bytes 10485760 | tf_op jit(solution)/shard_map/dot_general | solution.py:531
  480.3 10.9 %add_convert_fusion = bf16[2048,2048]{1,0:T(8,128)(2,1)} fusion(f32[2048,2048]{1,0:T(8,128)} %get-tuple-element.78, bf16[2048,512]{1,0:T(8,128)(2,1)S(1)} %copy-done.17, bf16[2048,512]{1,0:T(8,128)(2,1)} %param.17), kind=kOutput, calls=%fused_computation.16 | convolution fusion | flops 4303355904 | bytes 29360128 | tf_op jit(solution)/shard_map/dot_general | solution.py:590
  491.2 13.1 %collective-permute-done.1 = bf16[2048,256]{1,0:T(8,128)(2,1)} collective-permute-done((bf16[2048,256]{1,0:T(8,128)(2,1)}, bf16[2048,256]{1,0:T(8,128)(2,1)}, u32[]{:S(2)}, u32[]{:S(2)}) %collective-permute-start.1) | collective-permute-done | bytes 1048608 | tf_op jit(solution)/shard_map/ppermute | solution.py:532
  505.8 2.4 pad_maximum_fusion.2
  (156 shorter events, 28.4 us)
Async XLA Ops:
  0.6 74.7 %copy-start = (bf16[512,2048]{1,0:T(8,128)(2,1)S(1)}, bf16[512,2048]{1,0:T(8,128)(2,1)}, u32[]{:S(2)}) copy-start(bf16[512,2048]{1,0:T(8,128)(2,1)} %param.19) | copy-start | bytes 6291460
  8.4 16.8 %copy-start.52 = (s32[1,8,2]{1,2,0:T(2,128)S(1)}, s32[1,8,2]{1,2,0:T(2,128)}, u32[]{:S(2)}) copy-start(s32[1,8,2]{1,2,0:T(2,128)} %param.15) | copy-start | bytes 196
  25.2 4.4 copy-start.32
  25.2 131.8 %copy-start.30 = (f32[512]{0:T(512)}, f32[512]{0:T(512)S(1)}, u32[]{:S(2)}) copy-start(f32[512]{0:T(512)S(1)} %get-tuple-element.22) | copy-start | bytes 6148
  25.8 12.9 %copy-start.34 = (bf16[8,16]{1,0:T(8,128)(2,1)}, bf16[8,16]{1,0:T(8,128)(2,1)S(1)}, u32[]{:S(2)}) copy-start(bf16[8,16]{1,0:T(8,128)(2,1)S(1)} %get-tuple-element.71) | copy-start | bytes 772
  31.6 18.1 %copy-start.8 = (bf16[2048,512]{1,0:T(8,128)(2,1)}, bf16[2048,512]{1,0:T(8,128)(2,1)S(1)}, u32[]{:S(2)}) copy-start(bf16[2048,512]{1,0:T(8,128)(2,1)S(1)} %multiply_convert_fusion.5) | copy-start | bytes 6291460
  33.6 16.1 %copy-start.11 = (bf16[8,16,16,512]{3,2,1,0:T(8,128)(2,1)}, bf16[8,16,16,512]{3,2,1,0:T(8,128)(2,1)S(1)}, u32[]{:S(2)}) copy-start(bf16[8,16,16,512]{3,2,1,0:T(8,128)(2,1)S(1)} %get-tuple-element.57) | copy-start | bytes 6291460
  33.6 16.1 %copy-start.13 = (bf16[8,16,16,512]{3,2,1,0:T(8,128)(2,1)}, bf16[8,16,16,512]{3,2,1,0:T(8,128)(2,1)S(1)}, u32[]{:S(2)}) copy-start(bf16[8,16,16,512]{3,2,1,0:T(8,128)(2,1)S(1)} %get-tuple-element.58) | copy-start | bytes 6291460
  53.2 14.8 %copy-start.27 = (bf16[1,2048,256]{2,1,0:T(8,128)(2,1)S(1)}, bf16[1,2048,256]{2,1,0:T(8,128)(2,1)}, u32[]{:S(2)}) copy-start(bf16[1,2048,256]{2,1,0:T(8,128)(2,1)} %param.20) | copy-start | bytes 3145732
  53.3 19.1 %copy-start.44 = (f32[512]{0:T(512)S(1)}, f32[512]{0:T(512)}, u32[]{:S(2)}) copy-start(f32[512]{0:T(512)} %param.23) | copy-start | bytes 6148
  53.3 19.1 %copy-start.51 = (f32[512]{0:T(512)S(1)}, f32[512]{0:T(512)}, u32[]{:S(2)}) copy-start(f32[512]{0:T(512)} %param.24) | copy-start | bytes 6148
  68.0 96.6 %collective-permute-start = (bf16[2048,256]{1,0:T(8,128)(2,1)S(1)}, bf16[2048,256]{1,0:T(8,128)(2,1)}, u32[]{:S(2)}, u32[]{:S(2)}) collective-permute-start(bf16[2048,256]{1,0:T(8,128)(2,1)S(1)} %bitcast.171), channel_id=1, source_target_pairs={{0,16},{16,0},{1,17},{17,1},{2,18},{18,2},{3,19},{19,3},{4,20},{20... | collective-permute-start | bytes 3145736 | tf_op jit(solution)/shard_map/ppermute | solution.py:519
  71.0 93.6 %collective-permute-start.2 = (bf16[2048,256]{1,0:T(8,128)(2,1)}, bf16[2048,256]{1,0:T(8,128)(2,1)}, u32[]{:S(2)}, u32[]{:S(2)}) collective-permute-start(bf16[2048,256]{1,0:T(8,128)(2,1)} %dynamic-slice_bitcast_fusion), channel_id=1, source_target_pairs={{0,16},{16,0},{1,17},{17,1},{2,18},{18,2},{3,19},{19,3},{4,20},{20... | collective-permute-start | bytes 3145736 | tf_op jit(solution)/shard_map/ppermute | solution.py:504
  75.3 8.5 %copy-start.20 = (bf16[2048,512]{1,0:T(8,128)(2,1)}, bf16[2048,512]{1,0:T(8,128)(2,1)S(1)}, u32[]{:S(2)}) copy-start(bf16[2048,512]{1,0:T(8,128)(2,1)S(1)} %multiply_convert_fusion.4) | copy-start | bytes 6291460
  121.6 7.1 %copy-start.37 = (f32[2048]{0:T(1024)S(1)}, f32[2048]{0:T(1024)}, u32[]{:S(2)}) copy-start(f32[2048]{0:T(1024)} %param.25) | copy-start | bytes 24580
  121.6 7.1 %copy-start.48 = (f32[2048]{0:T(1024)S(1)}, f32[2048]{0:T(1024)}, u32[]{:S(2)}) copy-start(f32[2048]{0:T(1024)} %param.26) | copy-start | bytes 24580
  121.7 25.2 %slice-start = ((s8[4718592]{0:T(1024)(128)(4,1)}), s8[524288]{0:T(1024)(128)(4,1)S(1)}, s32[]{:S(2)}) async-start(s8[4718592]{0:T(1024)(128)(4,1)} %bitcast.140), calls=%async_computation | async-start | bytes 1048576
  128.7 18.1 %slice-start.1 = ((s8[4718592]{0:T(1024)(128)(4,1)}), s8[4194304]{0:T(1024)(128)(4,1)S(1)}, s32[]{:S(2)}) async-start(s8[4718592]{0:T(1024)(128)(4,1)} %bitcast.140), calls=%async_computation.1 | async-start | bytes 8388608
  149.1 8.4 %copy-start.29 = (f32[32,128]{1,0:T(8,128)S(1)}, f32[32,128]{1,0:T(8,128)}, u32[]{:S(2)}) copy-start(f32[32,128]{1,0:T(8,128)} %stats_2.1) | copy-start | bytes 49156
  206.5 12.3 %copy-start.36 = (f32[2048]{0:T(1024)}, f32[2048]{0:T(1024)S(1)}, u32[]{:S(2)}) copy-start(f32[2048]{0:T(1024)S(1)} %slice_bitcast_fusion.3) | copy-start | bytes 24580
  206.5 12.3 %copy-start.6 = (f32[2048,512]{1,0:T(8,128)S(1)}, f32[2048,512]{1,0:T(8,128)}, u32[]{:S(2)}) copy-start(f32[2048,512]{1,0:T(8,128)} %copy-done.5) | copy-start | bytes 12582916
  218.8 8.0 %copy-start.10 = (bf16[2048,2048]{1,0:T(8,128)(2,1)}, bf16[2048,2048]{1,0:T(8,128)(2,1)S(1)}, u32[]{:S(2)}) copy-start(bf16[2048,2048]{1,0:T(8,128)(2,1)S(1)} %multiply_convert_fusion) | copy-start | bytes 25165828
  239.4 10.1 %copy-start.46 = (f32[512]{0:T(512)}, f32[512]{0:T(512)S(1)}, u32[]{:S(2)}) copy-start(f32[512]{0:T(512)S(1)} %slice_bitcast_fusion.7) | copy-start | bytes 6148
  239.4 10.1 %copy-start.7 = (f32[2048,512]{1,0:T(8,128)S(1)}, f32[2048,512]{1,0:T(8,128)}, u32[]{:S(2)}) copy-start(f32[2048,512]{1,0:T(8,128)} %copy-done.5) | copy-start | bytes 12582916
  239.4 10.1 %copy-start.15 = (f32[2048,512]{1,0:T(8,128)S(1)}, f32[2048,512]{1,0:T(8,128)}, u32[]{:S(2)}) copy-start(f32[2048,512]{1,0:T(8,128)} %get-tuple-element.79) | copy-start | bytes 12582916
  254.9 15.4 %copy-start.26 = (bf16[512,3,512]{0,2,1:T(8,128)(2,1)S(1)}, bf16[512,3,512]{0,2,1:T(8,128)(2,1)}, u32[]{:S(2)}) copy-start(bf16[512,3,512]{0,2,1:T(8,128)(2,1)} %copy.39) | copy-start | bytes 4718596
  254.9 15.4 %copy-start.50 = (f32[8,16]{1,0:T(8,128)S(1)}, f32[8,16]{1,0:T(8,128)}, u32[]{:S(2)}) copy-start(f32[8,16]{1,0:T(8,128)} %get-tuple-element.65) | copy-start | bytes 1540
  270.3 7.9 %copy-start.22 = (bf16[8,16,16,512]{3,2,1,0:T(8,128)(2,1)S(1)}, bf16[8,16,16,512]{3,2,1,0:T(8,128)(2,1)}, u32[]{:S(2)}) copy-start(bf16[8,16,16,512]{3,2,1,0:T(8,128)(2,1)} %get-tuple-element.80) | copy-start | bytes 6291460
  270.3 7.9 %copy-start.23 = (bf16[8,16,16,512]{3,2,1,0:T(8,128)(2,1)S(1)}, bf16[8,16,16,512]{3,2,1,0:T(8,128)(2,1)}, u32[]{:S(2)}) copy-start(bf16[8,16,16,512]{3,2,1,0:T(8,128)(2,1)} %get-tuple-element.81) | copy-start | bytes 6291460
  270.3 7.8 %copy-start.24 = (bf16[512,3,512]{0,2,1:T(8,128)(2,1)S(1)}, bf16[512,3,512]{0,2,1:T(8,128)(2,1)}, u32[]{:S(2)}) copy-start(bf16[512,3,512]{0,2,1:T(8,128)(2,1)} %copy.37) | copy-start | bytes 4718596
  270.3 7.8 %copy-start.49 = (f32[8,16]{1,0:T(8,128)S(1)}, f32[8,16]{1,0:T(8,128)}, u32[]{:S(2)}) copy-start(f32[8,16]{1,0:T(8,128)} %get-tuple-element.67) | copy-start | bytes 1540
  278.2 4.9 copy-start.25
  283.1 6.3 %copy-start.4 = (f32[2048,512]{1,0:T(8,128)S(1)}, f32[2048,512]{1,0:T(8,128)}, u32[]{:S(2)}) copy-start(f32[2048,512]{1,0:T(8,128)} %copy-done.2) | copy-start | bytes 12582916
  283.1 6.3 %copy-start.31 = (f32[512]{0:T(512)S(1)}, f32[512]{0:T(512)}, u32[]{:S(2)}) copy-start(f32[512]{0:T(512)} %copy-done.30) | copy-start | bytes 6148
  283.1 6.3 %copy-start.33 = (f32[512]{0:T(512)S(1)}, f32[512]{0:T(512)}, u32[]{:S(2)}) copy-start(f32[512]{0:T(512)} %copy-done.32) | copy-start | bytes 6148
  283.1 6.3 %copy-start.39 = (f32[512]{0:T(512)S(1)}, f32[512]{0:T(512)}, u32[]{:S(2)}) copy-start(f32[512]{0:T(512)} %param.21) | copy-start | bytes 6148
  283.1 6.3 %copy-start.43 = (f32[512]{0:T(512)S(1)}, f32[512]{0:T(512)}, u32[]{:S(2)}) copy-start(f32[512]{0:T(512)} %param.22) | copy-start | bytes 6148
  289.4 16.5 %copy-start.45 = (f32[512]{0:T(512)S(1)}, f32[512]{0:T(512)}, u32[]{:S(2)}) copy-start(f32[512]{0:T(512)} %mul.319) | copy-start | bytes 6148
  305.9 4.8 copy-start.47
  305.9 18.8 %slice-start.2 = ((s8[8388608]{0:T(1024)(128)(4,1)}), s8[4194304]{0:T(1024)(128)(4,1)S(1)}, s32[]{:S(2)}) async-start(s8[8388608]{0:T(1024)(128)(4,1)} %bitcast.154), calls=%async_computation.2 | async-start | bytes 8388608
  310.7 12.6 %copy-start.16 = (bf16[2048,512]{1,0:T(8,128)(2,1)}, bf16[2048,512]{1,0:T(8,128)(2,1)S(1)}, u32[]{:S(2)}) copy-start(bf16[2048,512]{1,0:T(8,128)(2,1)S(1)} %multiply_convert_fusion.2) | copy-start | bytes 6291460
  310.8 12.6 %copy-start.14 = (bf16[1,2,8,256,256]{4,3,2,1,0:T(8,128)(2,1)S(1)}, bf16[1,2,8,256,256]{4,3,2,1,0:T(8,128)(2,1)}, u32[]{:S(2)}) copy-start(bf16[1,2,8,256,256]{4,3,2,1,0:T(8,128)(2,1)} %param.27) | copy-start | bytes 6291460
  310.8 14.0 %slice-start.3 = ((s8[8388608]{0:T(1024)(128)(4,1)}), s8[4194304]{0:T(1024)(128)(4,1)S(1)}, s32[]{:S(2)}) async-start(s8[8388608]{0:T(1024)(128)(4,1)} %bitcast.154), calls=%async_computation.3 | async-start | bytes 8388608
  454.7 11.5 %copy-start.19 = (bf16[2048,512]{1,0:T(8,128)(2,1)S(1)}, bf16[2048,512]{1,0:T(8,128)(2,1)}, u32[]{:S(2)}) copy-start(bf16[2048,512]{1,0:T(8,128)(2,1)} %get-tuple-element.24) | copy-start | bytes 6291460
  471.4 7.4 %copy-start.28 = (bf16[2048,512]{1,0:T(8,128)(2,1)S(1)}, bf16[2048,512]{1,0:T(8,128)(2,1)}, u32[]{:S(2)}) copy-start(bf16[2048,512]{1,0:T(8,128)(2,1)} %get-tuple-element.27) | copy-start | bytes 6291460
  471.4 8.9 %copy-start.17 = (bf16[2048,512]{1,0:T(8,128)(2,1)S(1)}, bf16[2048,512]{1,0:T(8,128)(2,1)}, u32[]{:S(2)}) copy-start(bf16[2048,512]{1,0:T(8,128)(2,1)} %copy-done.16) | copy-start | bytes 6291460
  478.5 25.8 %collective-permute-start.1 = (bf16[2048,256]{1,0:T(8,128)(2,1)}, bf16[2048,256]{1,0:T(8,128)(2,1)}, u32[]{:S(2)}, u32[]{:S(2)}) collective-permute-start(bf16[2048,256]{1,0:T(8,128)(2,1)} %convolution_convert_fusion.3), channel_id=1, source_target_pairs={{0,16},{16,0},{1,17},{17,1},{2,18},{18,2},{3,19},{19,3},{4,20},{20... | collective-permute-start | bytes 3145736 | tf_op jit(solution)/shard_map/ppermute | solution.py:532
  480.3 24.0 %copy-start.21 = (f32[2048,256]{1,0:T(8,128)S(1)}, f32[2048,256]{1,0:T(8,128)}, u32[]{:S(2)}) copy-start(f32[2048,256]{1,0:T(8,128)} %fusion.52) | copy-start | bytes 6291460
  (12 other events, 32.9 us)

commit v3 on v2

v3 whole, which is shorter than its diff:
```python
import functools
import math

import jax
import jax.numpy as jnp
from jax import lax
from jax.experimental import pallas as pl
from jax.experimental.pallas import tpu as pltpu
from jax.sharding import PartitionSpec as P

SIDE = 16
EPS = 1e-05
FLOOR = 0.1
SOFT = 0.25
ROOT_HALF = 0.7071067811865476
DENSITY = 0.3989422804014327
LOG2E = 1.4426950408889634
ERF_P = 0.3275911
ERF_A = (0.254829592, -0.284496736, 1.421413741, -1.453152027, 1.061405429)
ROWS_ROWS = (((0,), (0,)), ((), ()))
COLS_COLS = (((1,), (1,)), ((), ()))
MESH = pl.DeviceIdType.MESH
LOW = 4
VMEM_BYTES = 62 * 2**20


class Reduction:
    def __init__(self, grid, work, result, core, first, second, last, send, recv, far_send, far_recv, wide):
        self.grid, self.work, self.result, self.room = grid, work, result, (core, first, second, last)
        self.send, self.recv, self.far_send, self.far_recv = send, recv, far_send, far_recv
        self.wide = wide
        self.rows, self.cols = work.shape
        sizes = self.sizes(self.rows, self.cols, wide, grid.far)
        self.flat = sizes[3] == sizes[2] and grid.far > 1
        self.copies = {}

    @staticmethod
    def sizes(rows, cols, wide, far):
        if wide:
            core = (rows, cols // 2)
            first = (rows, cols // 8)
            second = (rows, cols // 16)
        else:
            core = (rows // 2, cols)
            first = (rows // 2, cols // 4)
            second = (rows // 4, cols // 4)
        if second[0] % (8 * far):
            return core, first, second, second
        return core, first, second, (second[0] // far, second[1])

    @staticmethod
    def room_shapes(rows, cols, wide, far):
        core, first, second, last = Reduction.sizes(rows, cols, wide, far)
        return [
            pltpu.VMEM(core, jnp.bfloat16),
            pltpu.VMEM((2,) + first, jnp.bfloat16),
            pltpu.VMEM((2,) + second, jnp.bfloat16),
            pltpu.VMEM((2, far) + last, jnp.bfloat16),
            pltpu.SemaphoreType.DMA((10,)),
            pltpu.SemaphoreType.DMA((10,)),
            pltpu.SemaphoreType.DMA((4, far)),
            pltpu.SemaphoreType.DMA((4, far)),
        ]

    def view(self, core, part=None, first=None, second=None, piece=None, done=False):
        grid = self.grid
        sizes = self.sizes(self.rows, self.cols, self.wide, grid.far)
        row = col = 0
        if self.wide:
            col = core * (self.cols // 2)
            shape = sizes[0]
            if part is not None:
                col = col + part * (self.cols // 4) + first * (self.cols // 8)
                shape = sizes[1]
            if second is not None:
                col = col + second * (self.cols // 16)
                shape = sizes[2]
        else:
            row = core * (self.rows // 2)
            shape = sizes[0]
            if part is not None:
                col = part * (self.cols // 2) + first * (self.cols // 4)
                shape = sizes[1]
            if second is not None:
                row = row + second * (self.rows // 4)
                shape = sizes[2]
        if piece is not None and not self.flat:
            row = row + piece * sizes[3][0]
            shape = sizes[3]
        if not isinstance(row, int):
            row = pl.multiple_of(row, shape[0] & -shape[0])
        if not isinstance(col, int):
            col = pl.multiple_of(col, 128)
        ref = self.result if done else self.work
        return ref.at[pl.ds(row, shape[0]), pl.ds(col, shape[1])]

    def swap(self, index, source, target, device):
        copy = pltpu.make_async_remote_copy(
            src_ref=source,
            dst_ref=target,
            send_sem=self.send.at[index],
            recv_sem=self.recv.at[index],
            device_id=device,
            device_id_type=MESH,
        )
        copy.start()
        self.copies[index] = copy

    def settle(self, *indices):
        for index in indices:
            self.copies.pop(index).wait()

    def add(self, target, sources):
        rows = target.shape[0]
        step = math.gcd(rows, 64)

        def one(i, carry):
            span = pl.ds(pl.multiple_of(i * step, step), step)
            total = sources[0][span].astype(jnp.float32)
            for source in sources[1:]:
                total = total + source[span].astype(jnp.float32)
            target[span] = total.astype(jnp.bfloat16)
            return carry

        lax.fori_loop(0, rows // step, one, 0)

    def join(self, mine, received):
        self.add(mine, [mine, received])

    def far_copy(self, part, step, back, inward):
        grid = self.grid
        bits = grid.bits(part)
        slot = lax.rem(grid.high + step, grid.far)
        owner = slot if inward else grid.high
        if back:
            source = self.view(grid.core, part, bits[0], bits[1], grid.high, True)
            target = self.view(grid.core, part, bits[0], bits[1], owner, True)
        else:
            source = self.view(grid.core, part, bits[0], bits[1], slot)
            target = self.room[3].at[part, owner]
        line = 2 * part + (1 if back else 0)
        return pltpu.make_async_remote_copy(
            src_ref=source,
            dst_ref=target,
            send_sem=self.far_send.at[line, step],
            recv_sem=self.far_recv.at[line, owner],
            device_id=(grid.task, slot * LOW + grid.low),
            device_id_type=MESH,
        )

    def far_start(self, back):
        for part in range(2):
            for step in range(1, self.grid.far):
                self.far_copy(part, step, back, False).start()

    def far_settle(self, back):
        for part in range(2):
            for step in range(1, self.grid.far):
                self.far_copy(part, step, back, True).wait_recv()
                self.far_copy(part, step, back, False).wait_send()

    def stage(self, index):
        grid = self.grid
        other = 1 - grid.core
        if index == 0:
            self.swap(0, self.view(other), self.room[0], grid.core_peer)
        elif index == 1:
            self.settle(0)
            self.join(self.view(grid.core), self.room[0])
            for part in range(2):
                bit = grid.bits(part)[0]
                self.swap(1 + part, self.view(grid.core, part, 1 - bit), self.room[1].at[part], grid.peers(part)[0])
        elif index == 2:
            self.settle(1, 2)
            for part in range(2):
                bits = grid.bits(part)
                self.join(self.view(grid.core, part, bits[0]), self.room[1].at[part])
                self.swap(
                    3 + part,
                    self.view(grid.core, part, bits[0], 1 - bits[1]),
                    self.room[2].at[part],
                    grid.peers(part)[1],
                )
        elif index == 3:
            self.settle(3, 4)
            for part in range(2):
                bits = grid.bits(part)
                self.join(self.view(grid.core, part, bits[0], bits[1]), self.room[2].at[part])
            self.far_start(False)
        elif index == 4:
            self.far_settle(False)
            for part in range(2):
                bits = grid.bits(part)
                mine = self.view(grid.core, part, bits[0], bits[1], grid.high)
                self.room[3][part, grid.high] = mine[...]
                self.add(
                    self.view(grid.core, part, bits[0], bits[1], grid.high, True),
                    [self.room[3].at[part, slot] for slot in range(grid.far)],
                )
            if not self.flat:
                self.far_start(True)
        elif index == 5:
            if not self.flat:
                self.far_settle(True)
            for part in range(2):
                bits = grid.bits(part)
                mine = self.view(grid.core, part, bits[0], bits[1], done=True)
                self.swap(5 + part, mine, mine, grid.peers(part)[1])
        elif index == 6:
            self.settle(5, 6)
            for part in range(2):
                mine = self.view(grid.core, part, grid.bits(part)[0], done=True)
                self.swap(7 + part, mine, mine, grid.peers(part)[0])
        elif index == 7:
            self.settle(7, 8)
            mine = self.view(grid.core, done=True)
            self.swap(9, mine, mine, grid.core_peer)
        elif index == 8:
            self.settle(9)


class Grid:
    def __init__(self, batch):
        self.task = lax.axis_index("task")
        place = lax.axis_index("batch")
        self.far = batch // LOW
        self.high = place // LOW
        self.low = lax.rem(place, LOW)
        self.core = lax.rem(place, 2)
        self.y = lax.rem(place // 2, 2)
        base = place - self.low
        self.core_peer = (self.task, base + self.y * 2 + (1 - self.core))
        self.x_peer = (1 - self.task, place)
        self.y_peer = (self.task, base + (1 - self.y) * 2 + self.core)

    def bits(self, part):
        return (self.task, self.y) if part == 0 else (self.y, self.task)

    def peers(self, part):
        return (self.x_peer, self.y_peer) if part == 0 else (self.y_peer, self.x_peer)

    def far_peers(self):
        return [
            (self.task, lax.rem(self.high + step, self.far) * LOW + self.low) for step in range(1, self.far)
        ]

    def meet(self):
        barrier = pltpu.get_barrier_semaphore()
        everyone = [self.core_peer, self.x_peer, self.y_peer] + self.far_peers()
        for device in everyone:
            pl.semaphore_signal(barrier, inc=1, device_id=device, device_id_type=MESH)
        return lambda: pl.semaphore_wait(barrier, len(everyone))


def sum_kernel(shapes, batch, *refs):
    count = len(shapes)
    sources, results = refs[:count], refs[count : 2 * count]
    refs = refs[2 * count :]
    works, refs = refs[:count], refs[count:]
    totals, refs = refs[:count], refs[count:]
    local, refs = refs[0], refs[1:]
    grid = Grid(batch)
    wait = grid.meet()
    chunks = []
    loads = []
    number = 0
    for item, (rows, cols, pieces, wide) in enumerate(shapes):
        height = rows // pieces
        for piece in range(pieces):
            span = pl.ds(piece * height, height)
            load = pltpu.make_async_copy(sources[item].at[span], works[item].at[span], local.at[number])
            load.start()
            store = pltpu.make_async_copy(totals[item].at[span], results[item].at[span], local.at[number])
            loads.append((load, store))
            room = refs[8 * number : 8 * number + 8]
            chunks.append(Reduction(grid, works[item].at[span], totals[item].at[span], *room, wide))
            number += 1
    wait()
    for wave in range(number + 8):
        for stage in range(8, -1, -1):
            chunk = wave - stage
            if 0 <= chunk < number:
                if stage == 0:
                    loads[chunk][0].wait()
                chunks[chunk].stage(stage)
                if stage == 8:
                    loads[chunk][1].start()
    for load, store in loads:
        store.wait()


def sum_all(arrays, pieces, wides, ident):
    batch = lax.axis_size("batch")
    far = batch // LOW
    shapes = [a.shape + (p, w) for a, p, w in zip(arrays, pieces, wides)]
    rooms = []
    for rows, cols, piece, wide in shapes:
        for _ in range(piece):
            rooms += Reduction.room_shapes(rows // piece, cols, wide, far)
    return pl.pallas_call(
        functools.partial(sum_kernel, shapes, batch),
        out_shape=[jax.ShapeDtypeStruct(a.shape, jnp.bfloat16) for a in arrays],
        in_specs=[pl.BlockSpec(memory_space=pl.ANY)] * len(arrays),
        out_specs=[pl.BlockSpec(memory_space=pl.ANY)] * len(arrays),
        scratch_shapes=[pltpu.VMEM(a.shape, jnp.bfloat16) for a in arrays + arrays]
        + [pltpu.SemaphoreType.DMA((sum(pieces),))]
        + rooms,
        compiler_params=pltpu.CompilerParams(
            collective_id=ident, has_side_effects=True, vmem_limit_bytes=VMEM_BYTES
        ),
        name="sum_all",
    )(*arrays)


class Exchange:
    def __init__(self, tasks, batch, near, far, near_send, near_recv, far_send, far_recv):
        place = lax.axis_index("batch")
        self.task = lax.axis_index("task")
        self.high = place // LOW
        self.low = lax.rem(place, LOW)
        self.near_size = tasks * LOW
        self.far_size = batch // LOW
        self.me_near = self.task * LOW + self.low
        self.near, self.far = near, far
        self.near_sems, self.far_sems = (near_send, near_recv), (far_send, far_recv)

    @staticmethod
    def scratch(tasks, batch, width):
        near_size, far_size = tasks * LOW, batch // LOW
        return [
            pltpu.VMEM((near_size + 1, 2, width), jnp.float32),
            pltpu.VMEM((far_size + 1, 2, width), jnp.float32),
            pltpu.SemaphoreType.DMA((near_size,)),
            pltpu.SemaphoreType.DMA((near_size,)),
            pltpu.SemaphoreType.DMA((far_size,)),
            pltpu.SemaphoreType.DMA((far_size,)),
        ]

    def near_peer(self, step):
        slot = lax.rem(self.me_near + step, self.near_size)
        return slot, (slot // LOW, self.high * LOW + lax.rem(slot, LOW))

    def far_peer(self, step):
        slot = lax.rem(self.high + step, self.far_size)
        return slot, (self.task, slot * LOW + self.low)

    def peers(self):
        near = [self.near_peer(step)[1] for step in range(1, self.near_size)]
        return near + [self.far_peer(step)[1] for step in range(1, self.far_size)]

    def greet(self):
        barrier = pltpu.get_barrier_semaphore()
        for device in self.peers():
            pl.semaphore_signal(barrier, inc=1, device_id=device, device_id_type=MESH)

    def met(self):
        pl.semaphore_wait(pltpu.get_barrier_semaphore(), self.near_size + self.far_size - 2)

    def hop(self, size, peer, me, held, sems):
        def copy(step, slot):
            return pltpu.make_async_remote_copy(
                src_ref=held.at[size],
                dst_ref=held.at[slot],
                send_sem=sems[0].at[step],
                recv_sem=sems[1].at[slot],
                device_id=peer(step)[1],
                device_id_type=MESH,
            )

        for step in range(1, size):
            copy(step, me).start()
        held[me] = held[size]
        for step in range(1, size):
            copy(step, peer(step)[0]).wait_recv()
        for step in range(1, size):
            copy(step, me).wait_send()
        return held[:size]

    def run(self, total, spread, rows, forward):
        self.near[self.near_size, 0:1] = total
        self.near[self.near_size, 1:2] = spread
        held = self.hop(self.near_size, self.near_peer, self.me_near, self.near, self.near_sems)
        total, spread = join(held, float(rows), forward)
        self.far[self.far_size, 0:1] = total
        self.far[self.far_size, 1:2] = spread
        held = self.hop(self.far_size, self.far_peer, self.high, self.far, self.far_sems)
        return join(held, float(rows * self.near_size), forward)


def join(held, share, forward):
    sums = held[:, 0, :]
    total = jnp.sum(sums, axis=0, keepdims=True)
    spread = jnp.sum(held[:, 1, :], axis=0, keepdims=True)
    if forward:
        groups = held.shape[0]
        away = sums * (1.0 / share) - total * (1.0 / (share * groups))
        spread = spread + share * jnp.sum(away * away, axis=0, keepdims=True)
    return total, spread


def stats_kernel(rows, forward, tasks, batch, stat_ref, vec_ref, out_ref, *scratch):
    exchange = Exchange(tasks, batch, *scratch)
    exchange.greet()
    count = rows * tasks * batch
    first = jnp.sum(stat_ref[:8], axis=0, keepdims=True)
    second = jnp.sum(stat_ref[8:16], axis=0, keepdims=True)
    exchange.met()
    out_ref[:8] = vec_ref[...]
    if forward:
        local = first + rows * stat_ref[16:17]
        total, spread = exchange.run(local, second - first * first * (1.0 / rows), rows, True)
        scale = lax.rsqrt(spread * (1.0 / count) + EPS)
        out_ref[0:1] = total * (1.0 / count)
        out_ref[1:2] = scale
        out_ref[4:5] = scale * vec_ref[2:3]
    else:
        total, spread = exchange.run(first, second, rows, False)
        out_ref[5:6] = total * (1.0 / count)
        out_ref[6:7] = spread * (1.0 / count)
        out_ref[8:9] = total
        out_ref[9:10] = spread


def reduce_stats(stat, vec, rows, forward, ident):
    tasks = lax.axis_size("task")
    batch = lax.axis_size("batch")
    width = stat.shape[1]
    return pl.pallas_call(
        functools.partial(stats_kernel, rows, forward, tasks, batch),
        out_shape=jax.ShapeDtypeStruct((16, width), jnp.float32),
        in_specs=[pl.BlockSpec(memory_space=pltpu.VMEM)] * 2,
        out_specs=pl.BlockSpec(memory_space=pltpu.VMEM),
        scratch_shapes=Exchange.scratch(tasks, batch, width),
        compiler_params=pltpu.CompilerParams(collective_id=ident, has_side_effects=True),
        name="stats_%d" % ident,
    )(stat, vec[:8])


def tail_and_bell(value):
    bell = jnp.exp2(value * value * (-0.5 * LOG2E))
    away = jnp.abs(value)
    ratio = 1.0 / (1.0 + away * (ERF_P * ROOT_HALF))
    poly = ERF_A[4]
    for factor in ERF_A[3::-1]:
        poly = poly * ratio + factor
    tail = 0.5 * poly * ratio * bell
    return jnp.where(value >= 0, 1.0 - tail, tail), bell


def fold(array):
    total = array[:8]
    for start in range(8, array.shape[0], 8):
        total = total + array[start : start + 8]
    return total


def crown_kernel(
    piece, h_ref, x_ref, thr_ref, cot_ref, cot_peer_ref, top_ref, top_peer_ref, vec_ref,
    out_ref, sent_ref, flow_ref, gradt_ref, stat_ref, z_ref, acc_ref,
):
    step = pl.program_id(0)
    rows, width = x_ref.shape
    half = cot_ref.shape[1]

    @pl.when(step == 0)
    def _():
        stat_ref[...] = jnp.zeros_like(stat_ref)
        acc_ref[...] = jnp.zeros_like(acc_ref)

    for start in range(0, width, piece):
        cols = pl.ds(start, piece)
        g_one = lax.dot_general(
            cot_ref[...], top_ref[cols], COLS_COLS, preferred_element_type=jnp.float32
        ).astype(jnp.bfloat16).astype(jnp.float32)
        g_two = lax.dot_general(
            cot_peer_ref[...], top_peer_ref[cols], COLS_COLS, preferred_element_type=jnp.float32
        ).astype(jnp.bfloat16).astype(jnp.float32)
        total = g_one + g_two
        size = jnp.abs(g_one) + jnp.abs(g_two)
        share = total / jnp.maximum(size, FLOOR)
        limit = thr_ref[:, cols].astype(jnp.float32)
        keep = jnp.clip((0.5 / SOFT) * share + ((0.5 / SOFT + 0.5) - limit * (1.0 / SOFT)), 0.0, 1.0)
        merged = 0.5 * (total - size) + keep * size
        normed = (h_ref[:, cols] - vec_ref[0:1, cols]) * vec_ref[1:2, cols]
        before = normed * vec_ref[2:3, cols] + vec_ref[3:4, cols] + x_ref[:, cols].astype(jnp.float32)
        phi, bell = tail_and_bell(before)
        z_ref[:, cols] = (before * phi).astype(jnp.bfloat16)
        flow = merged * (phi + before * bell * DENSITY)
        flow_ref[:, cols] = flow.astype(flow_ref.dtype)
        stat_ref[:8, cols] += fold(flow)
        stat_ref[8:, cols] += fold(flow * normed)
    out_ref[...] = jnp.dot(z_ref[...], top_ref[...], preferred_element_type=jnp.float32)
    sent_ref[...] = jnp.dot(z_ref[...], top_peer_ref[...], preferred_element_type=jnp.float32).astype(jnp.bfloat16)
    acc_ref[:half] += lax.dot_general(cot_ref[...], z_ref[...], ROWS_ROWS, preferred_element_type=jnp.float32)
    acc_ref[half:] += lax.dot_general(cot_peer_ref[...], z_ref[...], ROWS_ROWS, preferred_element_type=jnp.float32)

    @pl.when(step == pl.num_programs(0) - 1)
    def _():
        task = lax.axis_index("task")
        gradt_ref[pl.ds(task * half, half)] = acc_ref[:half].astype(jnp.bfloat16)
        gradt_ref[pl.ds((1 - task) * half, half)] = acc_ref[half:].astype(jnp.bfloat16)


def wide(mask, width):
    return jnp.concatenate([mask] * (width // mask.shape[1]), axis=1)


def gather_stats(stat_ref, hidden, first):
    @pl.when(first)
    def _():
        stat_ref[:16] = jnp.zeros_like(stat_ref[:16])
        mean = jnp.sum(hidden, axis=0, keepdims=True) / hidden.shape[0]
        stat_ref[16:] = jnp.broadcast_to(mean, stat_ref[16:].shape)

    away = hidden - stat_ref[16:17]
    stat_ref[:8] += fold(away)
    stat_ref[8:16] += fold(away * away)


def normal(hidden, vec_ref):
    return (hidden - vec_ref[0:1]) * vec_ref[1:2]


def squeeze_kernel(x_ref, w_ref, out_ref, stat_ref):
    hidden = jnp.dot(x_ref[...], w_ref[...], preferred_element_type=jnp.float32)
    out_ref[...] = hidden
    gather_stats(stat_ref, hidden, pl.program_id(0) == 0)


def mesh_kernel(h_ref, vec_ref, mask_ref, w_ref, out_ref, side_ref, stat_ref, pad_ref):
    rows, mid = h_ref.shape
    inner = pl.ds(SIDE, rows)
    before = normal(h_ref[...], vec_ref) * vec_ref[2:3] + vec_ref[3:4]
    phi, _ = tail_and_bell(before)
    low = (before * phi).astype(jnp.bfloat16)
    kept = low.astype(jnp.float32)
    left = wide(mask_ref[:, :128].astype(jnp.float32), mid)
    right = wide(mask_ref[:, 128:256].astype(jnp.float32), mid)

    @pl.when(pl.program_id(0) == 0)
    def _():
        pad_ref[:SIDE] = jnp.zeros_like(pad_ref[:SIDE])
        pad_ref[SIDE + rows :] = jnp.zeros_like(pad_ref[:SIDE])

    pad_ref[inner, :mid] = (pltpu.roll(kept, 1, 0) * left).astype(jnp.bfloat16)
    pad_ref[inner, mid : 2 * mid] = low
    pad_ref[inner, 2 * mid :] = (pltpu.roll(kept, rows - 1, 0) * right).astype(jnp.bfloat16)
    side_ref[...] = pad_ref[inner]
    above = wide(mask_ref[:, 256:384], 3 * mid)
    below = wide(mask_ref[:, 384:], 3 * mid)
    hidden = jnp.dot(pad_ref[inner], w_ref[3 * mid : 6 * mid], preferred_element_type=jnp.float32)
    hidden += jnp.dot(pad_ref[:rows] * above, w_ref[: 3 * mid], preferred_element_type=jnp.float32)
    hidden += jnp.dot(pad_ref[2 * SIDE :] * below, w_ref[6 * mid :], preferred_element_type=jnp.float32)
    out_ref[...] = hidden
    gather_stats(stat_ref, hidden, pl.program_id(0) == 0)


def widen_kernel(h_ref, vec_ref, w_ref, out_ref, low_ref, stat_ref):
    before = normal(h_ref[...], vec_ref) * vec_ref[2:3] + vec_ref[3:4]
    phi, _ = tail_and_bell(before)
    low = (before * phi).astype(jnp.bfloat16)
    low_ref[...] = low
    hidden = jnp.dot(low, w_ref[...], preferred_element_type=jnp.float32)
    out_ref[...] = hidden
    gather_stats(stat_ref, hidden, pl.program_id(0) == 0)


def norm_grad(upstream, normed, vec_ref):
    return vec_ref[4:5] * (upstream - vec_ref[5:6] - normed * vec_ref[6:7])


def act_slope(value):
    phi, bell = tail_and_bell(value)
    return phi + value * bell * DENSITY


def gather_flow(stat_ref, flow, normed, first):
    @pl.when(first)
    def _():
        stat_ref[...] = jnp.zeros_like(stat_ref)

    stat_ref[:8] += fold(flow)
    stat_ref[8:16] += fold(flow * normed)


def narrow_kernel(flow_ref, h_ref, vec_ref, two_ref, vectwo_ref, low_ref, w_ref, out_ref, grad_ref, stat_ref, acc_ref):
    first = pl.program_id(0) == 0
    dh = norm_grad(flow_ref[...].astype(jnp.float32), normal(h_ref[...], vec_ref), vec_ref).astype(jnp.bfloat16)
    dq = lax.dot_general(dh, w_ref[...], COLS_COLS, preferred_element_type=jnp.float32)
    normed = normal(two_ref[...], vectwo_ref)
    flow = dq * act_slope(normed * vectwo_ref[2:3] + vectwo_ref[3:4])
    out_ref[...] = flow
    gather_flow(stat_ref, flow, normed, first)
    part = lax.dot_general(low_ref[...], dh, ROWS_ROWS, preferred_element_type=jnp.float32)
    accumulate(acc_ref, grad_ref, part)


def accumulate(acc_ref, grad_ref, part):
    step = pl.program_id(0)
    last = pl.num_programs(0) - 1

    @pl.when(step == 0)
    def _():
        acc_ref[...] = part

    @pl.when((step > 0) & (step < last))
    def _():
        acc_ref[...] += part

    @pl.when(step == last)
    def _():
        grad_ref[...] = (acc_ref[...] + part).astype(jnp.bfloat16)


def unmesh_kernel(flow_ref, two_ref, vec_ref, one_ref, vecone_ref, side_ref, mask_ref, w_ref, out_ref, grad_ref, stat_ref, lane_ref, acc_ref):
    step = pl.program_id(0)
    last = pl.num_programs(0) - 1
    rows, mid = flow_ref.shape
    dh = norm_grad(flow_ref[...], normal(two_ref[...], vec_ref), vec_ref)
    above = wide(mask_ref[:, 256:384].astype(jnp.float32), mid)
    below = wide(mask_ref[:, 384:].astype(jnp.float32), mid)

    @pl.when(step == 0)
    def _():
        lane_ref[rows - SIDE :, :mid] = jnp.zeros((SIDE, mid), jnp.bfloat16)
        lane_ref[:SIDE, 2 * mid :] = jnp.zeros((SIDE, mid), jnp.bfloat16)

    lane_ref[: rows - SIDE, :mid] = (dh * above)[SIDE:].astype(jnp.bfloat16)
    lane_ref[:, mid : 2 * mid] = dh.astype(jnp.bfloat16)
    lane_ref[SIDE:, 2 * mid :] = (dh * below)[: rows - SIDE].astype(jnp.bfloat16)
    pieces = []
    for b in range(3):
        total = None
        for a in range(3):
            part = lax.dot_general(
                lane_ref[:, a * mid : (a + 1) * mid], w_ref[3 * a + b], COLS_COLS, preferred_element_type=jnp.float32
            )
            total = part if total is None else total + part
        pieces.append(total)
    left = wide(mask_ref[:, :128].astype(jnp.float32), mid)
    right = wide(mask_ref[:, 128:256].astype(jnp.float32), mid)
    dq = pieces[1] + pltpu.roll(pieces[0] * left, rows - 1, 0) + pltpu.roll(pieces[2] * right, 1, 0)
    normed = normal(one_ref[...], vecone_ref)
    flow = dq * act_slope(normed * vecone_ref[2:3] + vecone_ref[3:4])
    out_ref[...] = flow
    gather_flow(stat_ref, flow, normed, step == 0)
    for a in range(3):
        part = lax.dot_general(
            side_ref[...], lane_ref[:, a * mid : (a + 1) * mid], ROWS_ROWS, preferred_element_type=jnp.float32
        )
        span = pl.ds(a * 3 * mid, 3 * mid)
        accumulate(acc_ref.at[span], grad_ref.at[span], part)


def finish_kernel(flow_ref, one_ref, vec_ref, up_ref, x_ref, w_ref, out_ref, grad_ref, acc_ref):
    dh = norm_grad(flow_ref[...], normal(one_ref[...], vec_ref), vec_ref).astype(jnp.bfloat16)
    back = lax.dot_general(dh, w_ref[...], COLS_COLS, preferred_element_type=jnp.float32)
    out_ref[...] = (up_ref[...].astype(jnp.float32) + back).astype(jnp.bfloat16)
    accumulate(acc_ref, grad_ref, lax.dot_general(dh, x_ref[...], ROWS_ROWS, preferred_element_type=jnp.float32))


def tiled(kernel, tile, rows, moving, fixed, outs, stats, scratch, name):
    def block(array):
        return pl.BlockSpec((tile,) + array.shape[1:], lambda i: (i,) + (0,) * (len(array.shape) - 1))

    def whole(array):
        zeros = (0,) * len(array.shape)
        return pl.BlockSpec(array.shape, lambda i: zeros)

    return pl.pallas_call(
        kernel,
        grid=(rows // tile,),
        out_shape=outs + stats,
        in_specs=[block(a) if m else whole(a) for a, m in zip(moving, fixed)],
        out_specs=[block(a) for a in outs] + [whole(a) for a in stats],
        scratch_shapes=scratch,
        compiler_params=pltpu.CompilerParams(vmem_limit_bytes=VMEM_BYTES),
        name=name,
    )(*moving)


def shape32(*shape):
    return jax.ShapeDtypeStruct(shape, jnp.float32)


def shape16(*shape):
    return jax.ShapeDtypeStruct(shape, jnp.bfloat16)


def squeeze(flat_in, w_reduce, tile):
    rows, mid = flat_in.shape[0], w_reduce.shape[1]
    return tiled(squeeze_kernel, tile, rows, [flat_in, w_reduce], [1, 0], [shape32(rows, mid)], [shape32(24, mid)], [], "squeeze")


def mesh_forward(h_one, vec, masks, taps, tile):
    rows, mid = h_one.shape
    return tiled(
        mesh_kernel, tile, rows, [h_one, vec, masks, taps], [1, 0, 1, 0],
        [shape32(rows, mid), shape16(rows, 3 * mid)], [shape32(24, mid)],
        [pltpu.VMEM((tile + 2 * SIDE, 3 * mid), jnp.bfloat16)], "mesh_forward",
    )


def widen(h_two, vec, w_expand, tile):
    rows, mid = h_two.shape
    width = w_expand.shape[1]
    return tiled(
        widen_kernel, tile, rows, [h_two, vec, w_expand], [1, 0, 0],
        [shape32(rows, width), shape16(rows, mid)], [shape32(24, width)], [], "widen",
    )


def narrow(flow, h_three, vec_three, h_two, vec_two, q_two, w_expand, tile):
    rows, mid = h_two.shape
    width = w_expand.shape[1]
    return tiled(
        narrow_kernel, tile, rows, [flow, h_three, vec_three, h_two, vec_two, q_two, w_expand], [1, 1, 0, 1, 0, 1, 0],
        [shape32(rows, mid)], [shape16(mid, width), shape32(16, mid)], [pltpu.VMEM((mid, width), jnp.float32)], "narrow",
    )


def mesh_backward(flow, h_two, vec_two, h_one, vec_one, sides, masks, w_spatial, tile):
    rows, mid = h_two.shape
    return tiled(
        unmesh_kernel, tile, rows, [flow, h_two, vec_two, h_one, vec_one, sides, masks, w_spatial], [1, 1, 0, 1, 0, 1, 1, 0],
        [shape32(rows, mid)], [shape16(9 * mid, mid), shape32(16, mid)],
        [pltpu.VMEM((tile, 3 * mid), jnp.bfloat16), pltpu.VMEM((9 * mid, mid), jnp.float32)], "mesh_backward",
    )


def finish(flow, h_one, vec_one, up, flat_in, w_reduce, tile):
    rows, mid = h_one.shape
    width = flat_in.shape[1]
    return tiled(
        finish_kernel, tile, rows, [flow, h_one, vec_one, up, flat_in, w_reduce], [1, 1, 0, 1, 1, 0],
        [shape16(rows, width)], [shape16(mid, width)], [pltpu.VMEM((mid, width), jnp.float32)], "finish",
    )


def crown(h_three, flat_in, limits, cot, cot_peer, top, top_peer, vec, tile, piece):
    rows, width = flat_in.shape
    half = cot.shape[1]
    return tiled(
        functools.partial(crown_kernel, piece), tile, rows,
        [h_three, flat_in, limits, cot, cot_peer, top, top_peer, vec], [1, 1, 1, 1, 1, 0, 0, 0],
        [shape32(rows, half), shape16(rows, half), shape16(rows, width)],
        [shape16(2 * half, width), shape32(16, width)],
        [pltpu.VMEM((tile, width), jnp.bfloat16), pltpu.VMEM((2 * half, width), jnp.float32)],
        "crown",
    )


def body(
    inputs,
    crop_cuts,
    threshold,
    w_reduce,
    w_spatial,
    w_expand,
    w_heads,
    gain_one,
    bias_one,
    gain_two,
    bias_two,
    gain_three,
    bias_three,
    cotangent,
):
    low = jnp.bfloat16
    full = jnp.float32
    canvases, pixels, width = inputs.shape[1:]
    mid = w_reduce.shape[1]
    rows = canvases * pixels
    half = w_heads.shape[2]
    task = lax.axis_index("task")
    swap = [(0, 1), (1, 0)]
    cot = cotangent.reshape(2, rows, half)
    cot_mine = lax.dynamic_index_in_dim(cot, task, 0, keepdims=False)
    cot_sent = lax.dynamic_index_in_dim(cot, 1 - task, 0, keepdims=False)
    top_mine = w_heads[0]

    def params(gain, bias):
        zero = jnp.zeros_like(gain)
        return jnp.stack([zero, zero, gain, bias, zero, zero, zero, zero])

    lines = jnp.arange(SIDE, dtype=jnp.int32)
    cuts = crop_cuts.reshape(canvases, 2)
    from_above = jnp.logical_not((lines == cuts[:, 0:1]) | (lines == 0)[None, :])
    from_left = jnp.logical_not((lines == cuts[:, 1:2]) | (lines == 0)[None, :])
    from_below = jnp.pad(from_above[:, 1:], ((0, 0), (0, 1)))
    from_right = jnp.pad(from_left[:, 1:], ((0, 0), (0, 1)))
    shape = (canvases, SIDE, SIDE, 128)
    masks = jnp.concatenate(
        [jnp.broadcast_to(m[:, None, :, None], shape) for m in (from_left, from_right)]
        + [jnp.broadcast_to(m[:, :, None, None], shape) for m in (from_above, from_below)],
        axis=3,
    ).astype(low).reshape(rows, 512)

    flat_in = inputs.reshape(rows, width)
    h_one, stat = squeeze(flat_in, w_reduce, min(rows, 512))
    vec_one = reduce_stats(stat, params(gain_one, bias_one), rows, True, 0)
    cot_sent, vec_one = lax.optimization_barrier((cot_sent, vec_one))
    cot_peer = lax.ppermute(cot_sent, "task", swap)
    h_two, sides, stat = mesh_forward(h_one, vec_one, masks, w_spatial.reshape(9 * mid, mid), pixels)
    vec_two = reduce_stats(stat, params(gain_two, bias_two), rows, True, 1)
    top_sent, vec_two = lax.optimization_barrier((top_mine, vec_two))
    top_peer = lax.ppermute(top_sent, "task", swap)
    h_three, q_two, stat = widen(h_two, vec_two, w_expand, pixels)
    vec_three = reduce_stats(stat, params(gain_three, bias_three), rows, True, 2)
    out_mine, out_sent, flow, grad_heads, stat = crown(
        h_three, flat_in, threshold.reshape(rows, width), cot_mine, cot_peer, top_mine, top_peer, vec_three, pixels, 256
    )
    out_peer = lax.ppermute(out_sent, "task", swap).astype(full)
    first = jnp.where(task == 0, out_mine, out_peer)
    second = jnp.where(task == 0, out_peer, out_mine)
    head_out = jnp.stack([first, second]).reshape(1, 2, canvases, pixels, half)
    vec_three = reduce_stats(stat, vec_three, rows, False, 3)
    flow_two, grad_expand, stat = narrow(flow, h_three, vec_three, h_two, vec_two, q_two, w_expand, min(rows, 512))
    vec_two = reduce_stats(stat, vec_two, rows, False, 4)
    flow_one, grad_spatial, stat = mesh_backward(
        flow_two, h_two, vec_two, h_one, vec_one, sides, masks, w_spatial, min(rows, 512)
    )
    vec_one = reduce_stats(stat, vec_one, rows, False, 5)
    grad_inputs, grad_reduce = finish(flow_one, h_one, vec_one, flow, flat_in, w_reduce, min(rows, 512))
    grad_heads, grad_expand, grad_spatial, grad_reduce = sum_all(
        [grad_heads, grad_expand, grad_spatial, grad_reduce], [1, 1, 3, 1], [True, True, False, True], 6
    )
    grad_heads = lax.dynamic_slice_in_dim(grad_heads, task * half, half, axis=0)
    return (
        head_out,
        grad_inputs.reshape(inputs.shape),
        grad_reduce.T.astype(full),
        grad_spatial.reshape(w_spatial.shape).astype(full),
        grad_expand.astype(full),
        grad_heads.T.astype(full)[None],
        vec_one[9],
        vec_one[8],
        vec_two[9],
        vec_two[8],
        vec_three[9],
        vec_three[8],
    )


def solution(mesh):
    in_specs = (
        P("task", "batch", None, None),
        P("task", "batch", None),
        P("task", "batch", None, None),
        P(),
        P(),
        P(),
        P("task", None, None),
        P(),
        P(),
        P(),
        P(),
        P(),
        P(),
        P("task", None, "batch", None, None),
    )
    out_specs = (
        P("task", None, "batch", None, None),
        P("task", "batch", None, None),
        P(),
        P(),
        P(),
        P("task", None, None),
        P(),
        P(),
        P(),
        P(),
        P(),
        P(),
    )
    return jax.shard_map(body, mesh=mesh, in_specs=in_specs, out_specs=out_specs, check_vma=False)
```

time: 515 us -> 434 us (0.84)
  Pallas kernels: 191 us -> 367 us
  matrix products: 159 us -> 0 us
  other arithmetic: 88.1 us -> 21.9 us
  local copies, waits for them, and re-layouts: 53.1 us -> 20 us
    pallas_call x0 -> x7, Pallas kernels: none -> 170 us  [tiled(): pl.pallas_call(kernel, grid=(rows // tile,), out_shape=outs + stats, in_s...]
    dot_general x18 -> x0, matrix products: 159 us -> none  [the longest x1 28.7 us: body(): lax.dot_general(cot_peer, heads_peer, COLS_COLS, preferred_element_type=f...]
    convert_element_type x10 -> x4, other arithmetic: 47.1 us -> 16.4 us  [the longest x1 7.52 us: body(): grad_spatial.reshape(w_spatial.shape).astype(full)]
    convert_element_type x2 -> x0, local copies, waits for them, and re-layouts: 27 us -> none  [body(): grad_spatial.reshape(3, mid, 3, mid).transpose(2, 0, 1, 3)]
    reduce_sum x4 -> x0, other arithmetic: 12.5 us -> none  [the longest x3 8.52 us: norm_forward(): spread = jnp.sum(jnp.square(hidden - total / rows), axis=0)]
    transpose x4 -> x0, local copies, waits for them, and re-layouts: 10.1 us -> none  [body(): across[:, b].transpose(1, 0, 2).reshape(mid, 3 * mid)]
    concatenate x7 -> x0, other arithmetic: 8.64 us -> none  [the longest x1 5.03 us: body(): jnp.concatenate([moved(q_one, 0, -1) * by_col(from_left), q_one, moved(q_...]
    mul x6 -> x0, other arithmetic: 7.07 us -> none  [the longest x1 4.09 us: body(): moved(sides, -1, 0) * by_row(from_above)]
  transfers between devices with their start and end apart: 3 -> 3, of which waited for: 1 -> 1; matrix products, arithmetic and copies ran while one was open for 15% -> 4% of each run, Pallas kernels for 6% -> 11%
where the time goes in v3:
time: 434 us; the launch traced here: 427 us
  Pallas kernels  367 us (85%)
  other arithmetic  21.9 us (5%)
  local copies, waits for them, and re-layouts  20 us (5%)
  waiting for transfers between devices  13.5 us (3%)
    pallas_call x7, Pallas kernels, tiled(): pl.pallas_call(kernel, grid=(rows // tile,), out_shape=outs + stats, in_s...  170 us
    pallas_call x1, Pallas kernels, sum_all(): pl.pallas_call(functools.partial(sum_kernel, shapes, batch), out_shape=[j...  108 us
    pallas_call x6, Pallas kernels, reduce_stats(): pl.pallas_call(functools.partial(stats_kernel, rows, forward, tasks, batc...  89.3 us
    ppermute x1, waiting for transfers between devices, body(): out_peer = lax.ppermute(out_sent, 'task', swap).astype(full)  13.5 us
  transfers between devices with their start and end apart: 3, of which 1 were waited for; matrix products, arithmetic and copies ran while one was open for 4% of the time, Pallas kernels for 11%

profile of v3, /device:TPU:0, one launch (start us, length us, event | category | flops | bytes accessed | tf_op | source)
XLA Modules:
  0.0 426.7 jit_solution(16961256290345552605)
XLA Ops:
  0.7 0.1 pad.26.clone
  0.8 9.3 %squeeze.38 = (f32[2048,512]{1,0:T(8,128)}, f32[24,512]{1,0:T(8,128)}) custom-call(bf16[2048,2048]{1,0:T(8,128)(2,1)} %bitcast.37, bf16[2048,512]{1,0:T(8,128)(2,1)} %w_ref.9), custom_call_target="tpu_custom_call" | custom-call | tf_op jit(solution)/shard_map/squeeze/pallas_call | solution.py:670
  10.1 0.7 maximum_maximum_fusion.2
  10.8 13.0 %stats_0.1.vec_ref.vecone_ref = f32[16,512]{1,0:T(8,128)} custom-call(f32[24,512]{1,0:T(8,128)} %get-tuple-element.42.stat_ref, f32[8,512]{1,0:T(8,128)} %get-tuple-element.93.vec_ref), custom_call_target="tpu_custom_call" | custom-call | tf_op jit(solution)/shard_map/stats_0/pallas_call | solution.py:428
  23.9 3.0 dynamic-slice_bitcast_fusion
  26.9 0.1 fusion.1
  27.1 0.1 broadcast_in_dim.54
  27.2 0.1 broadcast_in_dim.59
  27.3 0.1 broadcast_in_dim.60
  27.5 0.1 broadcast_in_dim.51
  27.5 0.1 broadcast_in_dim.56
  27.6 0.1 broadcast_in_dim.57
  27.7 0.3 broadcast_in_dim.55
  28.1 0.3 broadcast_in_dim.61
  28.4 0.3 broadcast_in_dim.52
  28.8 0.3 broadcast_in_dim.58
  29.1 2.0 add_convert_fusion.mask_ref
  31.1 22.2 %mesh_forward.1 = (f32[2048,512]{1,0:T(8,128)}, bf16[2048,1536]{1,0:T(8,128)(2,1)}, f32[24,512]{1,0:T(8,128)}) custom-call(f32[2048,512]{1,0:T(8,128)} %get-tuple-element.41.h_ref.one_ref, f32[16,512]{1,0:T(8,128)} %stats_0.1.vec_ref.vecone_ref, bf16[2048,512]{1,0:T(8,128)(2,1)} %add_convert_fusion.mask_ref, bf16[4608,512]{1,0:T(8,128)(2,1)} %bitcast.40), custom_call_target="tpu_custom_call" | custom-call | tf_op jit(solution)/shard_map/mesh_forward/pallas_call | solution.py:670
  53.3 11.1 %stats_1.1.vec_ref.vectwo_ref = f32[16,512]{1,0:T(8,128)} custom-call(f32[24,512]{1,0:T(8,128)} %get-tuple-element.45.stat_ref, f32[8,512]{1,0:T(8,128)} %get-tuple-element.92.vec_ref), custom_call_target="tpu_custom_call" | custom-call | tf_op jit(solution)/shard_map/stats_1/pallas_call | solution.py:428
  64.5 0.8 collective-permute-start.1
  65.2 1.3 collective-permute-start
  66.6 0.6 slice.48.vec_ref
  67.2 1.3 slice.47.vec_ref
  68.5 14.6 %widen.1 = (f32[2048,2048]{1,0:T(8,128)}, bf16[2048,512]{1,0:T(8,128)(2,1)}, f32[24,2048]{1,0:T(8,128)}) custom-call(f32[2048,512]{1,0:T(8,128)} %get-tuple-element.44.h_ref.two_ref, f32[16,512]{1,0:T(8,128)} %stats_1.1.vec_ref.vectwo_ref, bf16[512,2048]{1,0:T(8,128)(2,1)} %w_ref.7), custom_call_target="tpu_custom_call" | custom-call | tf_op jit(solution)/shard_map/widen/pallas_call | solution.py:670
  83.1 0.7 maximum_maximum_fusion.vec_ref
  83.8 33.8 %stats_2.1.vec_ref = f32[16,2048]{1,0:T(8,128)} custom-call(f32[24,2048]{1,0:T(8,128)} %get-tuple-element.50.stat_ref, f32[8,2048]{1,0:T(8,128)} %maximum_maximum_fusion.vec_ref), custom_call_target="tpu_custom_call" | custom-call | tf_op jit(solution)/shard_map/stats_2/pallas_call | solution.py:428
  117.6 1.5 slice.46.vec_ref
  119.1 43.9 %crown.1 = (f32[2048,256]{1,0:T(8,128)}, bf16[2048,256]{1,0:T(8,128)(2,1)}, bf16[2048,2048]{1,0:T(8,128)(2,1)}, bf16[512,2048]{1,0:T(8,128)(2,1)}, f32[16,2048]{1,0:T(8,128)}) custom-call(f32[2048,2048]{1,0:T(8,128)} %get-tuple-element.47.h_ref, bf16[2048,2048]{1,0:T(8,128)(2,1)} %bitcast.38, bf16[2048,2048]{1,0:T(8,128)(2,1)} %bitcast.41, ...), custom_call_target="tpu_custom_call" | custom-call | tf_op jit(solution)/shard_map/crown/pallas_call | solution.py:670
  162.9 11.0 %stats_3.1.vec_ref = f32[16,2048]{1,0:T(8,128)} custom-call(f32[16,2048]{1,0:T(8,128)} %get-tuple-element.54.stat_ref, f32[8,2048]{1,0:T(8,128)} %slice.46.vec_ref), custom_call_target="tpu_custom_call" | custom-call | tf_op jit(solution)/shard_map/stats_3/pallas_call | solution.py:428
  173.9 22.6 %narrow.1 = (f32[2048,512]{1,0:T(8,128)}, bf16[512,2048]{1,0:T(8,128)(2,1)}, f32[16,512]{1,0:T(8,128)}) custom-call(bf16[2048,2048]{1,0:T(8,128)(2,1)} %get-tuple-element.53.flow_ref.up_ref, f32[2048,2048]{1,0:T(8,128)} %get-tuple-element.47.h_ref, f32[16,2048]{1,0:T(8,128)} %stats_3.1.vec_ref, f32[2048,512]{1,0:T(8,128)} %get-tuple-element.44.h_ref.two_ref, ...), custom_call_target="tpu_custom_call" | custom-call | tf_op jit(solution)/shard_map/narrow/pallas_call | solution.py:670
  196.5 10.3 %stats_4.1.vec_ref = f32[16,512]{1,0:T(8,128)} custom-call(f32[16,512]{1,0:T(8,128)} %get-tuple-element.57.stat_ref, f32[8,512]{1,0:T(8,128)} %slice.47.vec_ref), custom_call_target="tpu_custom_call" | custom-call | tf_op jit(solution)/shard_map/stats_4/pallas_call | solution.py:428
  206.8 39.6 %mesh_backward.1 = (f32[2048,512]{1,0:T(8,128)}, bf16[4608,512]{1,0:T(8,128)(2,1)}, f32[16,512]{1,0:T(8,128)}) custom-call(f32[2048,512]{1,0:T(8,128)} %get-tuple-element.56.flow_ref, f32[2048,512]{1,0:T(8,128)} %get-tuple-element.44.h_ref.two_ref, f32[16,512]{1,0:T(8,128)} %stats_4.1.vec_ref, f32[2048,512]{1,0:T(8,128)} %get-tuple-element.41.h_ref.one_ref, ...), custom_call_target="tpu_custom_call" | custom-call | tf_op jit(solution)/shard_map/mesh_backward/pallas_call | solution.py:670
  246.4 10.1 %stats_5.1.vec_ref = f32[16,512]{1,0:T(8,128)} custom-call(f32[16,512]{1,0:T(8,128)} %get-tuple-element.60.stat_ref, f32[8,512]{1,0:T(8,128)} %slice.48.vec_ref), custom_call_target="tpu_custom_call" | custom-call | tf_op jit(solution)/shard_map/stats_5/pallas_call | solution.py:428
  256.5 17.8 %finish.1 = (bf16[2048,2048]{1,0:T(8,128)(2,1)}, bf16[512,2048]{1,0:T(8,128)(2,1)}) custom-call(f32[2048,512]{1,0:T(8,128)} %get-tuple-element.59.flow_ref, f32[2048,512]{1,0:T(8,128)} %get-tuple-element.41.h_ref.one_ref, f32[16,512]{1,0:T(8,128)} %stats_5.1.vec_ref, bf16[2048,2048]{1,0:T(8,128)(2,1)} %get-tuple-element.53.flow_ref.up_ref, ...), custom_call_target="tpu_custom_call" | custom-call | tf_op jit(solution)/shard_map/finish/pallas_call | solution.py:670
  274.3 108.2 %sum_all.1 = (bf16[512,2048]{1,0:T(8,128)(2,1)}, bf16[512,2048]{1,0:T(8,128)(2,1)}, bf16[4608,512]{1,0:T(8,128)(2,1)}, bf16[512,2048]{1,0:T(8,128)(2,1)}) custom-call(bf16[512,2048]{1,0:T(8,128)(2,1)} %get-tuple-element.62.refs_0_, bf16[512,2048]{1,0:T(8,128)(2,1)} %get-tuple-element.63.refs_1_, bf16[4608,512]{1,0:T(8,128)(2,1)} %get-tuple-element.64.refs_2_, ...), custom_call_target="tpu_custom_call" | custom-call | tf_op jit(solution)/shard_map/sum_all/pallas_call | solution.py:300
  382.5 7.5 %convert.4 = f32[9,512,512]{2,1,0:T(8,128)} convert(bf16[9,512,512]{2,1,0:T(8,128)(2,1)} %bitcast.44) | non-fusion elementwise | flops 2359296 | bytes 14155776 | tf_op jit(solution)/shard_map/convert_element_type | solution.py:833
  390.1 2.5 convert_bitcast_fusion
  392.6 5.3 %copy.26 = f32[2048,512]{1,0:T(8,128)} copy(f32[2048,512]{0,1:T(8,128)} %convert_bitcast_fusion) | data formatting | bytes 8388608
  397.9 0.3 collective-permute-start.2
  398.2 1.5 convert_bitcast_fusion.1
  399.7 1.8 copy.27
  401.5 4.3 %convert_element_type.35 = f32[512,2048]{1,0:T(8,128)} convert(bf16[512,2048]{1,0:T(8,128)(2,1)} %get-tuple-element.68) | non-fusion elementwise | flops 1048576 | bytes 6291456 | tf_op jit(solution)/shard_map/convert_element_type | solution.py:834
  405.8 1.4 fusion.6
  407.2 1.4 fusion.5
  408.5 1.5 fusion.4
  410.1 13.5 %collective-permute-done.2 = bf16[2048,256]{1,0:T(8,128)(2,1)S(1)} collective-permute-done((bf16[2048,256]{1,0:T(8,128)(2,1)}, bf16[2048,256]{1,0:T(8,128)(2,1)S(1)}, u32[]{:S(2)}, u32[]{:S(2)}) %collective-permute-start.2) | collective-permute-done | bytes 1048608 | tf_op jit(solution)/shard_map/ppermute | solution.py:813
  423.6 0.4 convert_select_fusion.1
  424.0 2.3 pad_maximum_fusion
  (35 shorter events, 0.3 us)
Async XLA Ops:
  0.8 9.3 %copy-start.6 = (f32[512]{0:T(512)S(1)}, f32[512]{0:T(512)}, u32[]{:S(2)}) copy-start(f32[512]{0:T(512)} %param.24) | copy-start | bytes 6148
  0.8 9.3 %copy-start.7 = (f32[512]{0:T(512)S(1)}, f32[512]{0:T(512)}, u32[]{:S(2)}) copy-start(f32[512]{0:T(512)} %param.23) | copy-start | bytes 6148
  0.8 9.3 %copy-start.8 = (f32[512]{0:T(512)S(1)}, f32[512]{0:T(512)}, u32[]{:S(2)}) copy-start(f32[512]{0:T(512)} %param.22) | copy-start | bytes 6148
  0.8 9.3 %copy-start.9 = (f32[512]{0:T(512)S(1)}, f32[512]{0:T(512)}, u32[]{:S(2)}) copy-start(f32[512]{0:T(512)} %param.21) | copy-start | bytes 6148
  23.9 3.0 copy-start.10
  31.1 33.3 %copy-start.2 = (bf16[1,2048,256]{2,1,0:T(8,128)(2,1)S(1)}, bf16[1,2048,256]{2,1,0:T(8,128)(2,1)}, u32[]{:S(2)}) copy-start(bf16[1,2048,256]{2,1,0:T(8,128)(2,1)} %param.20) | copy-start | bytes 3145732
  31.1 35.4 %copy-start.3 = (f32[16,512]{1,0:T(8,128)S(1)}, f32[16,512]{1,0:T(8,128)}, u32[]{:S(2)}) copy-start(f32[16,512]{1,0:T(8,128)} %stats_0.1.vec_ref.vecone_ref) | copy-start | bytes 98308
  64.5 54.6 %collective-permute-start.1 = (bf16[2048,256]{1,0:T(8,128)(2,1)S(1)}, bf16[2048,256]{1,0:T(8,128)(2,1)}, u32[]{:S(2)}, u32[]{:S(2)}) collective-permute-start(bf16[2048,256]{1,0:T(8,128)(2,1)S(1)} %bitcast.47), channel_id=1, source_target_pairs={{0,16},{16,0},{1,17},{17,1},{2,18},{18,2},{3,19},{19,3},{4,20},{20... | collective-permute-start | bytes 3145736 | tf_op jit(solution)/shard_map/ppermute | solution.py:807
  65.2 53.9 %collective-permute-start = (bf16[2048,256]{1,0:T(8,128)(2,1)}, bf16[2048,256]{1,0:T(8,128)(2,1)}, u32[]{:S(2)}, u32[]{:S(2)}) collective-permute-start(bf16[2048,256]{1,0:T(8,128)(2,1)} %get-tuple-element.48), channel_id=1, source_target_pairs={{0,16},{16,0},{1,17},{17,1},{2,18},{18,2},{3,19},{19,3},{4,20},{20... | collective-permute-start | bytes 3145736 | tf_op jit(solution)/shard_map/ppermute | solution.py:803
  68.5 14.6 %copy-start.4 = (f32[2048]{0:T(1024)S(1)}, f32[2048]{0:T(1024)}, u32[]{:S(2)}) copy-start(f32[2048]{0:T(1024)} %param.26) | copy-start | bytes 24580
  68.5 14.6 %copy-start.5 = (f32[2048]{0:T(1024)S(1)}, f32[2048]{0:T(1024)}, u32[]{:S(2)}) copy-start(f32[2048]{0:T(1024)} %param.25) | copy-start | bytes 24580
  382.5 7.5 %copy-start = (bf16[512,2048]{1,0:T(8,128)(2,1)S(1)}, bf16[512,2048]{1,0:T(8,128)(2,1)}, u32[]{:S(2)}) copy-start(bf16[512,2048]{1,0:T(8,128)(2,1)} %get-tuple-element.66) | copy-start | bytes 6291460
  397.9 25.6 %collective-permute-start.2 = (bf16[2048,256]{1,0:T(8,128)(2,1)}, bf16[2048,256]{1,0:T(8,128)(2,1)S(1)}, u32[]{:S(2)}, u32[]{:S(2)}) collective-permute-start(bf16[2048,256]{1,0:T(8,128)(2,1)} %get-tuple-element.52), channel_id=1, source_target_pairs={{0,16},{16,0},{1,17},{17,1},{2,18},{18,2},{3,19},{19,3},{4,20},{20... | collective-permute-start | bytes 3145736 | tf_op jit(solution)/shard_map/ppermute | solution.py:813
  401.5 22.1 %copy-start.1 = (f32[2048,256]{1,0:T(8,128)S(1)}, f32[2048,256]{1,0:T(8,128)}, u32[]{:S(2)}) copy-start(f32[2048,256]{1,0:T(8,128)} %get-tuple-element.51) | copy-start | bytes 6291460
